TPU v7x, 32 devices: a whole 2x2x4 slice. The times are simulated.
32 devices in a mesh: seq: 8 (over z, core), tp: 4 (over y, x).
Axes of the slice: x: 2, y: 2, z: 4, core: 2. Of those that a mesh axis runs over, the one named last changes fastest.
Arguments:
- q_heads: bfloat16 [1024, 4096], P('seq', 'tp'), may hold values from -200 to 200
- k_heads: bfloat16 [1024, 4096], P('seq', 'tp'), may hold values from -4 to 4
- v_heads: bfloat16 [1024, 4096], P('seq', 'tp'), may hold values from -5 to 5
- grad_attn: bfloat16 [1024, 4096], P('seq', 'tp'), may hold values from -5 to 5
- attn_out: bfloat16 [1024, 4096], P('seq', 'tp'), may hold values from -5 to 5
- gate_q: bfloat16 [1024, 8192], P('seq', 'tp'), may hold values from -5 to 5
- feat_k: bfloat16 [1024, 8192], P('seq', 'tp'), may hold values from -5 to 5
- feat_v: bfloat16 [1024, 8192], P('seq', 'tp'), may hold values from -5 to 5
- conv_out: bfloat16 [1024, 8192], P('seq', 'tp'), may hold values from -5 to 5
- grad_y: bfloat16 [1024, 8192], P('seq', 'tp'), may hold values from -5 to 5
- filters: float32 [64, 128], replicated, may hold values from -0.5 to 0.5
Outputs:
- grad_q: bfloat16 [1024, 4096], P('seq', 'tp')
- grad_k: bfloat16 [1024, 4096], P('seq', 'tp')
- grad_v: bfloat16 [1024, 4096], P('seq', 'tp')
- grad_gate: bfloat16 [1024, 8192], P('seq', 'tp')
- grad_feat_k: bfloat16 [1024, 8192], P('seq', 'tp')
- grad_feat_v: bfloat16 [1024, 8192], P('seq', 'tp')
- grad_filters: float32 [64, 128], replicated
All inputs are finite; a program needn't handle non-finite values.
Results may differ from a plain program's by a relative error of at most 0.014.
Values may be sent and summed in bfloat16 or wider, within the bound.
A program may use at most 64 MiB of HBM per device.

v0:
```python
import jax
import jax.numpy as jnp
from jax import lax
from jax.sharding import PartitionSpec as P

HEADS = 32


def from_behind(value, axis, steps):
    count = lax.axis_size(axis)
    leading, last = (max(0, -steps), min(count, count - steps))
    return lax.ppermute(value, axis, [(source, source + steps) for source in range(leading, last)])


def wire_parts(x):
    high = x.astype(jnp.bfloat16)
    back = lax.optimization_barrier(high).astype(jnp.float32)
    low = (x - back).astype(jnp.bfloat16)
    return (high, low)


def local(
    q_heads,
    k_heads,
    v_heads,
    grad_attn,
    attn_out,
    gate_q,
    feat_k,
    feat_v,
    conv_out,
    grad_y,
    filters,
):
    rows = q_heads.shape[0]
    heads_here = HEADS // lax.axis_size("tp")
    width = q_heads.shape[1] // heads_here
    scale = 1.0 / width**0.5
    shards = lax.axis_size("seq")
    place = lax.axis_index("seq")
    queries = q_heads.reshape(rows, heads_here, width)
    upstream = grad_attn.reshape(rows, heads_here, width)
    keys_here = k_heads.reshape(rows, heads_here, width)
    values_here = v_heads.reshape(rows, heads_here, width)
    delta = jnp.sum(
        upstream.astype(jnp.float32)
        * attn_out.reshape(rows, heads_here, width).astype(jnp.float32),
        axis=2,
    )
    delta_heads = delta.T
    diagonal = jnp.arange(rows)[:, None] >= jnp.arange(rows)[None, :]

    def query_tile(state, key_piece, value_piece, live):
        top, total, acc = state
        count = key_piece.shape[0]
        key_block = key_piece.reshape(count, heads_here, width)
        value_block = value_piece.reshape(count, heads_here, width)
        scores = (
            jnp.einsum("qhd,khd->hqk", queries, key_block, preferred_element_type=jnp.float32)
            * scale
        )
        top_new = jnp.maximum(top, jnp.max(jnp.where(live[None], scores, -1e30), axis=2))
        weights = jnp.where(live[None], jnp.exp(scores - top_new[:, :, None]), 0.0)
        decay = jnp.exp(top - top_new)
        dprob = jnp.einsum(
            "qhd,khd->hqk", upstream, value_block, preferred_element_type=jnp.float32
        )
        term = jnp.einsum(
            "hqk,khd->qhd",
            weights * (dprob - delta_heads[:, :, None]),
            key_block.astype(jnp.float32),
            precision=lax.Precision.HIGHEST,
        )
        return (top_new, total * decay + jnp.sum(weights, axis=2), acc * decay.T[:, :, None] + term)

    zero_rows = jnp.zeros((rows, heads_here, width), jnp.float32)
    state = (
        jnp.full((heads_here, rows), -1e30, jnp.float32),
        jnp.zeros((heads_here, rows), jnp.float32),
        zero_rows,
    )
    state = query_tile(state, k_heads, v_heads, diagonal)

    def relay_keys(back, carry):
        inner, moving = carry
        moving = from_behind((moving[0], moving[1]), "seq", 1)
        valid = place >= back
        live = jnp.broadcast_to(valid, (rows, rows))
        inner = query_tile(inner, moving[0], moving[1], live)
        return (inner, moving)

    state, moved = lax.fori_loop(1, shards, relay_keys, (state, (k_heads, v_heads)))
    top, total, acc = state
    lse = (top + jnp.log(total)).T
    grad_query = acc * (1.0 / total).T[:, :, None] * scale
    lse_high, lse_low = wire_parts(lse)
    delta_high, delta_low = wire_parts(delta)
    stats = jnp.stack([lse_high, lse_low, delta_high, delta_low], axis=1)

    def key_tile(inner, query_piece, upstream_piece, stat_piece, live):
        key_grad, value_grad = inner
        count = query_piece.shape[0]
        query_block = query_piece.reshape(count, heads_here, width)
        upstream_block = upstream_piece.reshape(count, heads_here, width)
        lse_w = stat_piece[:, 0].astype(jnp.float32) + stat_piece[:, 1].astype(jnp.float32)
        delta_w = stat_piece[:, 2].astype(jnp.float32) + stat_piece[:, 3].astype(jnp.float32)
        scores = (
            jnp.einsum("qhd,khd->hqk", query_block, keys_here, preferred_element_type=jnp.float32)
            * scale
        )
        probs = jnp.where(live[None], jnp.exp(scores - lse_w.T[:, :, None]), 0.0)
        dprob = jnp.einsum(
            "qhd,khd->hqk", upstream_block, values_here, preferred_element_type=jnp.float32
        )
        dscore = probs * (dprob - delta_w.T[:, :, None])
        value_grad = value_grad + jnp.einsum(
            "hqk,qhd->khd",
            probs.astype(jnp.bfloat16),
            upstream_block,
            preferred_element_type=jnp.float32,
        )
        key_grad = key_grad + jnp.einsum(
            "hqk,qhd->khd",
            dscore.astype(jnp.bfloat16),
            query_block,
            preferred_element_type=jnp.float32,
        )
        return (key_grad, value_grad)

    grads = (zero_rows, zero_rows)
    grads = key_tile(grads, q_heads, grad_attn, stats, diagonal)

    def relay_queries(back, carry):
        inner, moving = carry
        moving = from_behind((moving[0], moving[1], moving[2]), "seq", -1)
        valid = place + back <= shards - 1
        live = jnp.broadcast_to(valid, (rows, rows))
        inner = key_tile(inner, moving[0], moving[1], moving[2], live)
        return (inner, moving)

    grads, moved = lax.fori_loop(1, shards, relay_queries, (grads, (q_heads, grad_attn, stats)))
    key_grad, value_grad = grads
    grad_q = grad_query.astype(jnp.bfloat16).reshape(rows, heads_here * width)
    grad_k = (key_grad * scale).astype(jnp.bfloat16).reshape(rows, heads_here * width)
    grad_v = value_grad.astype(jnp.bfloat16).reshape(rows, heads_here * width)
    span_taps = filters.shape[1]
    groups = filters.shape[0]
    channels = gate_q.shape[1]
    dz = (grad_y.astype(jnp.float32) * gate_q.astype(jnp.float32)).astype(jnp.bfloat16)
    rim = from_behind(dz[: span_taps - 1], "seq", -1)
    grad_gate = (grad_y.astype(jnp.float32) * conv_out.astype(jnp.float32)).astype(jnp.bfloat16)
    padded = jnp.concatenate([dz, rim], axis=0).astype(jnp.float32)
    taps = jnp.tile(filters.T, (1, channels // groups))
    mixed = feat_k.astype(jnp.float32) * feat_v.astype(jnp.float32)
    numbers = ("NWC", "WIO", "NWC")
    dw = lax.conv_general_dilated(
        padded[None],
        taps[:, None, :],
        (1,),
        "VALID",
        dimension_numbers=numbers,
        feature_group_count=channels,
        precision=lax.Precision.HIGHEST,
    )[0]
    local_terms = lax.conv_general_dilated(
        padded[None],
        mixed[:, None, :],
        (1,),
        "VALID",
        dimension_numbers=numbers,
        feature_group_count=channels,
        precision=lax.Precision.HIGHEST,
    )[0]
    grad_feat_k = (dw * feat_v.astype(jnp.float32)).astype(jnp.bfloat16)
    grad_feat_v = (dw * feat_k.astype(jnp.float32)).astype(jnp.bfloat16)
    local_terms = jnp.sum(local_terms.reshape(span_taps, channels // groups, groups), axis=1).T
    filter_total = lax.psum(local_terms, ("seq", "tp"))
    count_all = rows * shards * channels * lax.axis_size("tp") / groups
    grad_filters = filter_total * (1.0 / count_all**0.5)
    return (grad_q, grad_k, grad_v, grad_gate, grad_feat_k, grad_feat_v, grad_filters)


def solution(mesh):
    in_specs = (
        P("seq", "tp"),
        P("seq", "tp"),
        P("seq", "tp"),
        P("seq", "tp"),
        P("seq", "tp"),
        P("seq", "tp"),
        P("seq", "tp"),
        P("seq", "tp"),
        P("seq", "tp"),
        P("seq", "tp"),
        P(),
    )
    out_specs = (
        P("seq", "tp"),
        P("seq", "tp"),
        P("seq", "tp"),
        P("seq", "tp"),
        P("seq", "tp"),
        P("seq", "tp"),
        P(),
    )
    return jax.shard_map(local, mesh=mesh, in_specs=in_specs, out_specs=out_specs, check_vma=False)
```

profile of v0, /device:TPU:0, one launch (start us, length us, event | category | flops | bytes accessed | tf_op | source)
XLA Modules:
  0.0 252.8 jit_solution(9573498819342594499)
XLA Ops:
  0.7 2.7 %fusion.19 = (bf16[128,2048]{1,0:T(8,128)(2,1)}, bf16[128,2048]{1,0:T(8,128)(2,1)}) fusion(bf16[128,2048]{1,0:T(8,128)(2,1)} %param.24, bf16[128,2048]{1,0:T(8,128)(2,1)} %param.20, bf16[128,2048]{1,0:T(8,128)(2,1)} %param.23), kind=kLoop, calls=%fused_computation.41 | loop fusion | flops 1835008 | bytes 2621440 | tf_op jit(solution)/shard_map/convert_element_type | solution.py:149
  3.4 1.4 collective-permute-start.5
  8.7 79.7 %while.42 = (s32[]{:T(128)}, f32[8,128]{1,0:T(8,128)S(1)}, f32[8,128]{1,0:T(8,128)S(1)}, f32[128,8,128]{2,0,1:T(8,128)S(1)}, bf16[128,1024]{0,1:T(8,128)(2,1)S(1...) while((s32[]{:T(128)}, f32[8,128]{1,0:T(8,128)S(1)}, ...), condition=%wide.region_6.7_spmd, body=%wide.region_3.6_spmd.sunk | while | flops 270011392 | bytes 8196297 | solution.py:92
  8.7 3.0 %collective-permute-start = (bf16[128,1024]{0,1:T(8,128)(2,1)S(1)}, bf16[128,1024]{0,1:T(8,128)(2,1)S(1)}, u32[]{:S(2)}, u32[]{:S(2)}) collective-permute-start(bf16[128,1024]{0,1:T(8,128)(2,1)S(1)} %get-tuple-element.618), channel_id=1, source_target_pairs={{0,4},{4,8},{8,12},{12,16},{16,20},{20,24},{24,28},{1,5},{5,9},{9,... | collective-permute-start | bytes 786440 | tf_op jit(solution)/shard_map/while/body/eval_jaxpr/ppermute | solution.py:12
  11.7 4.6 %collective-permute-start.1 = (bf16[128,1024]{0,1:T(8,128)(2,1)S(1)}, bf16[128,1024]{0,1:T(8,128)(2,1)S(1)}, u32[]{:S(2)}, u32[]{:S(2)}) collective-permute-start(bf16[128,1024]{0,1:T(8,128)(2,1)S(1)} %get-tuple-element.619), channel_id=1, source_target_pairs={{0,4},{4,8},{8,12},{12,16},{16,20},{20,24},{24,28},{1,5},{5,9},{9,... | collective-permute-start | bytes 786440 | tf_op jit(solution)/shard_map/while/body/eval_jaxpr/ppermute | solution.py:12
  17.8 0.7 fusion.102
  18.6 5.0 %collective-permute-start = (bf16[128,1024]{0,1:T(8,128)(2,1)S(1)}, bf16[128,1024]{0,1:T(8,128)(2,1)S(1)}, u32[]{:S(2)}, u32[]{:S(2)}) collective-permute-start(bf16[128,1024]{0,1:T(8,128)(2,1)S(1)} %get-tuple-element.618), channel_id=1, source_target_pairs={{0,4},{4,8},{8,12},{12,16},{16,20},{20,24},{24,28},{1,5},{5,9},{9,... | collective-permute-start | bytes 786440 | tf_op jit(solution)/shard_map/while/body/eval_jaxpr/ppermute | solution.py:12
  23.5 4.4 %collective-permute-start.1 = (bf16[128,1024]{0,1:T(8,128)(2,1)S(1)}, bf16[128,1024]{0,1:T(8,128)(2,1)S(1)}, u32[]{:S(2)}, u32[]{:S(2)}) collective-permute-start(bf16[128,1024]{0,1:T(8,128)(2,1)S(1)} %get-tuple-element.619), channel_id=1, source_target_pairs={{0,4},{4,8},{8,12},{12,16},{16,20},{20,24},{24,28},{1,5},{5,9},{9,... | collective-permute-start | bytes 786440 | tf_op jit(solution)/shard_map/while/body/eval_jaxpr/ppermute | solution.py:12
  30.2 5.0 %collective-permute-start = (bf16[128,1024]{0,1:T(8,128)(2,1)S(1)}, bf16[128,1024]{0,1:T(8,128)(2,1)S(1)}, u32[]{:S(2)}, u32[]{:S(2)}) collective-permute-start(bf16[128,1024]{0,1:T(8,128)(2,1)S(1)} %get-tuple-element.618), channel_id=1, source_target_pairs={{0,4},{4,8},{8,12},{12,16},{16,20},{20,24},{24,28},{1,5},{5,9},{9,... | collective-permute-start | bytes 786440 | tf_op jit(solution)/shard_map/while/body/eval_jaxpr/ppermute | solution.py:12
  35.2 4.4 %collective-permute-start.1 = (bf16[128,1024]{0,1:T(8,128)(2,1)S(1)}, bf16[128,1024]{0,1:T(8,128)(2,1)S(1)}, u32[]{:S(2)}, u32[]{:S(2)}) collective-permute-start(bf16[128,1024]{0,1:T(8,128)(2,1)S(1)} %get-tuple-element.619), channel_id=1, source_target_pairs={{0,4},{4,8},{8,12},{12,16},{16,20},{20,24},{24,28},{1,5},{5,9},{9,... | collective-permute-start | bytes 786440 | tf_op jit(solution)/shard_map/while/body/eval_jaxpr/ppermute | solution.py:12
  41.8 5.0 %collective-permute-start = (bf16[128,1024]{0,1:T(8,128)(2,1)S(1)}, bf16[128,1024]{0,1:T(8,128)(2,1)S(1)}, u32[]{:S(2)}, u32[]{:S(2)}) collective-permute-start(bf16[128,1024]{0,1:T(8,128)(2,1)S(1)} %get-tuple-element.618), channel_id=1, source_target_pairs={{0,4},{4,8},{8,12},{12,16},{16,20},{20,24},{24,28},{1,5},{5,9},{9,... | collective-permute-start | bytes 786440 | tf_op jit(solution)/shard_map/while/body/eval_jaxpr/ppermute | solution.py:12
  46.8 4.4 %collective-permute-start.1 = (bf16[128,1024]{0,1:T(8,128)(2,1)S(1)}, bf16[128,1024]{0,1:T(8,128)(2,1)S(1)}, u32[]{:S(2)}, u32[]{:S(2)}) collective-permute-start(bf16[128,1024]{0,1:T(8,128)(2,1)S(1)} %get-tuple-element.619), channel_id=1, source_target_pairs={{0,4},{4,8},{8,12},{12,16},{16,20},{20,24},{24,28},{1,5},{5,9},{9,... | collective-permute-start | bytes 786440 | tf_op jit(solution)/shard_map/while/body/eval_jaxpr/ppermute | solution.py:12
  53.5 5.0 %collective-permute-start = (bf16[128,1024]{0,1:T(8,128)(2,1)S(1)}, bf16[128,1024]{0,1:T(8,128)(2,1)S(1)}, u32[]{:S(2)}, u32[]{:S(2)}) collective-permute-start(bf16[128,1024]{0,1:T(8,128)(2,1)S(1)} %get-tuple-element.618), channel_id=1, source_target_pairs={{0,4},{4,8},{8,12},{12,16},{16,20},{20,24},{24,28},{1,5},{5,9},{9,... | collective-permute-start | bytes 786440 | tf_op jit(solution)/shard_map/while/body/eval_jaxpr/ppermute | solution.py:12
  58.4 4.4 %collective-permute-start.1 = (bf16[128,1024]{0,1:T(8,128)(2,1)S(1)}, bf16[128,1024]{0,1:T(8,128)(2,1)S(1)}, u32[]{:S(2)}, u32[]{:S(2)}) collective-permute-start(bf16[128,1024]{0,1:T(8,128)(2,1)S(1)} %get-tuple-element.619), channel_id=1, source_target_pairs={{0,4},{4,8},{8,12},{12,16},{16,20},{20,24},{24,28},{1,5},{5,9},{9,... | collective-permute-start | bytes 786440 | tf_op jit(solution)/shard_map/while/body/eval_jaxpr/ppermute | solution.py:12
  65.1 5.0 %collective-permute-start = (bf16[128,1024]{0,1:T(8,128)(2,1)S(1)}, bf16[128,1024]{0,1:T(8,128)(2,1)S(1)}, u32[]{:S(2)}, u32[]{:S(2)}) collective-permute-start(bf16[128,1024]{0,1:T(8,128)(2,1)S(1)} %get-tuple-element.618), channel_id=1, source_target_pairs={{0,4},{4,8},{8,12},{12,16},{16,20},{20,24},{24,28},{1,5},{5,9},{9,... | collective-permute-start | bytes 786440 | tf_op jit(solution)/shard_map/while/body/eval_jaxpr/ppermute | solution.py:12
  70.1 4.4 %collective-permute-start.1 = (bf16[128,1024]{0,1:T(8,128)(2,1)S(1)}, bf16[128,1024]{0,1:T(8,128)(2,1)S(1)}, u32[]{:S(2)}, u32[]{:S(2)}) collective-permute-start(bf16[128,1024]{0,1:T(8,128)(2,1)S(1)} %get-tuple-element.619), channel_id=1, source_target_pairs={{0,4},{4,8},{8,12},{12,16},{16,20},{20,24},{24,28},{1,5},{5,9},{9,... | collective-permute-start | bytes 786440 | tf_op jit(solution)/shard_map/while/body/eval_jaxpr/ppermute | solution.py:12
  76.7 5.0 %collective-permute-start = (bf16[128,1024]{0,1:T(8,128)(2,1)S(1)}, bf16[128,1024]{0,1:T(8,128)(2,1)S(1)}, u32[]{:S(2)}, u32[]{:S(2)}) collective-permute-start(bf16[128,1024]{0,1:T(8,128)(2,1)S(1)} %get-tuple-element.618), channel_id=1, source_target_pairs={{0,4},{4,8},{8,12},{12,16},{16,20},{20,24},{24,28},{1,5},{5,9},{9,... | collective-permute-start | bytes 786440 | tf_op jit(solution)/shard_map/while/body/eval_jaxpr/ppermute | solution.py:12
  81.7 4.4 %collective-permute-start.1 = (bf16[128,1024]{0,1:T(8,128)(2,1)S(1)}, bf16[128,1024]{0,1:T(8,128)(2,1)S(1)}, u32[]{:S(2)}, u32[]{:S(2)}) collective-permute-start(bf16[128,1024]{0,1:T(8,128)(2,1)S(1)} %get-tuple-element.619), channel_id=1, source_target_pairs={{0,4},{4,8},{8,12},{12,16},{16,20},{20,24},{24,28},{1,5},{5,9},{9,... | collective-permute-start | bytes 786440 | tf_op jit(solution)/shard_map/while/body/eval_jaxpr/ppermute | solution.py:12
  89.8 87.0 %while.43 = (s32[]{:T(128)}, f32[128,8,128]{2,0,1:T(8,128)S(1)}, f32[128,8,128]{2,0,1:T(8,128)S(1)}, bf16[128,1024]{0,1:T(8,128)(2,1)S(1)}, bf16[128,1024]{0,1:T...) while((s32[]{:T(128)}, f32[128,8,128]{2,0,1:T(8,128)S(1)}, ...), condition=%wide.region_8.9_spmd, body=%wide.region_7.8_spmd.sunk | while | flops 135403520 | bytes 8462587 | solution.py:141
  89.8 1.3 collective-permute-start.2
  91.1 1.3 collective-permute-start.3
  92.4 1.3 collective-permute-start.4
  93.7 3.6 %collective-permute-done.3 = bf16[128,4,8]{0,2,1:T(8,128)(2,1)S(1)} collective-permute-done((bf16[128,4,8]{0,2,1:T(8,128)(2,1)S(1)}, bf16[128,4,8]{0,2,1:T(8,128)(2,1)S(1)}, u32[]{:S(2)}, u32[]{:S(2)}) %collective-permute-start.3) | collective-permute-done | bytes 8224 | tf_op jit(solution)/shard_map/while/body/eval_jaxpr/ppermute | solution.py:12
  97.7 1.9 collective-permute-done.4
  100.6 1.3 collective-permute-start.2
  101.9 1.3 collective-permute-start.3
  103.2 1.3 collective-permute-start.4
  104.5 6.1 %collective-permute-done.3 = bf16[128,4,8]{0,2,1:T(8,128)(2,1)S(1)} collective-permute-done((bf16[128,4,8]{0,2,1:T(8,128)(2,1)S(1)}, bf16[128,4,8]{0,2,1:T(8,128)(2,1)S(1)}, u32[]{:S(2)}, u32[]{:S(2)}) %collective-permute-start.3) | collective-permute-done | bytes 8224 | tf_op jit(solution)/shard_map/while/body/eval_jaxpr/ppermute | solution.py:12
  111.0 1.9 collective-permute-done.4
  113.9 1.3 collective-permute-start.2
  115.2 1.3 collective-permute-start.3
  116.5 1.3 collective-permute-start.4
  117.8 5.4 %collective-permute-done.3 = bf16[128,4,8]{0,2,1:T(8,128)(2,1)S(1)} collective-permute-done((bf16[128,4,8]{0,2,1:T(8,128)(2,1)S(1)}, bf16[128,4,8]{0,2,1:T(8,128)(2,1)S(1)}, u32[]{:S(2)}, u32[]{:S(2)}) %collective-permute-start.3) | collective-permute-done | bytes 8224 | tf_op jit(solution)/shard_map/while/body/eval_jaxpr/ppermute | solution.py:12
  123.6 1.9 collective-permute-done.4
  126.5 1.3 collective-permute-start.2
  127.8 1.3 collective-permute-start.3
  129.1 1.3 collective-permute-start.4
  130.4 5.4 %collective-permute-done.3 = bf16[128,4,8]{0,2,1:T(8,128)(2,1)S(1)} collective-permute-done((bf16[128,4,8]{0,2,1:T(8,128)(2,1)S(1)}, bf16[128,4,8]{0,2,1:T(8,128)(2,1)S(1)}, u32[]{:S(2)}, u32[]{:S(2)}) %collective-permute-start.3) | collective-permute-done | bytes 8224 | tf_op jit(solution)/shard_map/while/body/eval_jaxpr/ppermute | solution.py:12
  136.1 1.9 collective-permute-done.4
  139.1 1.3 collective-permute-start.2
  140.4 1.3 collective-permute-start.3
  141.7 1.3 collective-permute-start.4
  143.0 5.3 %collective-permute-done.3 = bf16[128,4,8]{0,2,1:T(8,128)(2,1)S(1)} collective-permute-done((bf16[128,4,8]{0,2,1:T(8,128)(2,1)S(1)}, bf16[128,4,8]{0,2,1:T(8,128)(2,1)S(1)}, u32[]{:S(2)}, u32[]{:S(2)}) %collective-permute-start.3) | collective-permute-done | bytes 8224 | tf_op jit(solution)/shard_map/while/body/eval_jaxpr/ppermute | solution.py:12
  148.7 1.9 collective-permute-done.4
  151.6 1.3 collective-permute-start.2
  152.9 1.3 collective-permute-start.3
  154.2 1.3 collective-permute-start.4
  155.5 5.3 %collective-permute-done.3 = bf16[128,4,8]{0,2,1:T(8,128)(2,1)S(1)} collective-permute-done((bf16[128,4,8]{0,2,1:T(8,128)(2,1)S(1)}, bf16[128,4,8]{0,2,1:T(8,128)(2,1)S(1)}, u32[]{:S(2)}, u32[]{:S(2)}) %collective-permute-start.3) | collective-permute-done | bytes 8224 | tf_op jit(solution)/shard_map/while/body/eval_jaxpr/ppermute | solution.py:12
  161.2 1.9 collective-permute-done.4
  164.2 1.3 collective-permute-start.2
  165.5 1.3 collective-permute-start.3
  166.8 1.3 collective-permute-start.4
  168.1 5.3 %collective-permute-done.3 = bf16[128,4,8]{0,2,1:T(8,128)(2,1)S(1)} collective-permute-done((bf16[128,4,8]{0,2,1:T(8,128)(2,1)S(1)}, bf16[128,4,8]{0,2,1:T(8,128)(2,1)S(1)}, u32[]{:S(2)}, u32[]{:S(2)}) %collective-permute-start.3) | collective-permute-done | bytes 8224 | tf_op jit(solution)/shard_map/while/body/eval_jaxpr/ppermute | solution.py:12
  173.8 1.9 collective-permute-done.4
  176.9 0.8 copy.239
  177.7 0.8 copy.238
  178.6 0.8 copy.197
  179.4 0.9 copy_bitcast_fusion.2
  180.3 1.3 maximum_bitcast_fusion
  181.6 11.6 %fusion.15 = f32[1,128,2048]{2,0,1:T(1,128)S(1)} fusion(f32[128,1,2048]{2,1,0:T(1,128)S(1)} %copy.197, bf16[1,255,2048]{2,1,0:T(8,128)(2,1)S(1)} %maximum_bitcast_fusion), kind=kOutput, calls=%fused_computation.28 | convolution fusion | flops 402653184 | bytes 3141632 | tf_op jit(solution)/shard_map/conv_general_dilated | solution.py:156
  193.2 1.6 fusion.21
  194.7 11.7 %fusion.13 = f32[1,128,2048]{2,0,1:T(1,128)S(1)} fusion(bf16[1,255,2048]{2,1,0:T(8,128)(2,1)S(1)} %maximum_bitcast_fusion, f32[128,1,2048]{2,0,1:T(8,128)S(1)} %get-tuple-element.462), kind=kOutput, calls=%fused_computation.26 | convolution fusion | flops 402653184 | bytes 3141632 | tf_op jit(solution)/shard_map/conv_general_dilated | solution.py:165
  206.4 0.7 copy.200
  207.2 44.9 %psum.7 = f32[64,128]{1,0:T(8,128)S(1)} all-reduce(f32[64,128]{1,0:T(8,128)S(1)} %bitcast.177), channel_id=1, replica_groups=mesh['seq'=8,'tp'=4] {'seq','tp'}, use_global_device_ids=true, to_apply=%region_10.11 | all-reduce | flops 8192 | bytes 65536 | tf_op jit(solution)/shard_map/psum | solution.py:177
  (190 shorter events, 29.8 us)
Async XLA Ops:
  0.6 4.2 %copy-start.6 = (bf16[128,1024]{1,0:T(8,128)(2,1)S(1)}, bf16[128,1024]{1,0:T(8,128)(2,1)}, u32[]{:S(2)}) copy-start(bf16[128,1024]{1,0:T(8,128)(2,1)} %param.18) | copy-start | bytes 786436
  0.6 4.3 %copy-start.7 = (bf16[128,1024]{1,0:T(8,128)(2,1)S(1)}, bf16[128,1024]{1,0:T(8,128)(2,1)}, u32[]{:S(2)}) copy-start(bf16[128,1024]{1,0:T(8,128)(2,1)} %param.19) | copy-start | bytes 786436
  3.3 2.0 copy-start.8
  3.4 176.9 %collective-permute-start.5 = (bf16[127,2048]{1,0:T(8,128)(2,1)}, bf16[127,2048]{1,0:T(8,128)(2,1)}, u32[]{:S(2)}, u32[]{:S(2)}) collective-permute-start(bf16[127,2048]{1,0:T(8,128)(2,1)} %bitcast.110), channel_id=1, source_target_pairs={{4,0},{8,4},{12,8},{16,12},{20,16},{24,20},{28,24},{5,1},{9,5},{13... | collective-permute-start | bytes 1560584 | tf_op jit(solution)/shard_map/ppermute | solution.py:12
  5.6 1.0 copy-start.9
  5.8 1.0 copy-start.10
  6.2 1.8 copy-start
  6.7 1.1 copy-start.2
  8.7 7.7 %collective-permute-start = (bf16[128,1024]{0,1:T(8,128)(2,1)S(1)}, bf16[128,1024]{0,1:T(8,128)(2,1)S(1)}, u32[]{:S(2)}, u32[]{:S(2)}) collective-permute-start(bf16[128,1024]{0,1:T(8,128)(2,1)S(1)} %get-tuple-element.618), channel_id=1, source_target_pairs={{0,4},{4,8},{8,12},{12,16},{16,20},{20,24},{24,28},{1,5},{5,9},{9,... | collective-permute-start | bytes 786440 | tf_op jit(solution)/shard_map/while/body/eval_jaxpr/ppermute | solution.py:12
  11.7 5.7 %collective-permute-start.1 = (bf16[128,1024]{0,1:T(8,128)(2,1)S(1)}, bf16[128,1024]{0,1:T(8,128)(2,1)S(1)}, u32[]{:S(2)}, u32[]{:S(2)}) collective-permute-start(bf16[128,1024]{0,1:T(8,128)(2,1)S(1)} %get-tuple-element.619), channel_id=1, source_target_pairs={{0,4},{4,8},{8,12},{12,16},{16,20},{20,24},{24,28},{1,5},{5,9},{9,... | collective-permute-start | bytes 786440 | tf_op jit(solution)/shard_map/while/body/eval_jaxpr/ppermute | solution.py:12
  18.6 9.4 %collective-permute-start = (bf16[128,1024]{0,1:T(8,128)(2,1)S(1)}, bf16[128,1024]{0,1:T(8,128)(2,1)S(1)}, u32[]{:S(2)}, u32[]{:S(2)}) collective-permute-start(bf16[128,1024]{0,1:T(8,128)(2,1)S(1)} %get-tuple-element.618), channel_id=1, source_target_pairs={{0,4},{4,8},{8,12},{12,16},{16,20},{20,24},{24,28},{1,5},{5,9},{9,... | collective-permute-start | bytes 786440 | tf_op jit(solution)/shard_map/while/body/eval_jaxpr/ppermute | solution.py:12
  23.5 5.5 %collective-permute-start.1 = (bf16[128,1024]{0,1:T(8,128)(2,1)S(1)}, bf16[128,1024]{0,1:T(8,128)(2,1)S(1)}, u32[]{:S(2)}, u32[]{:S(2)}) collective-permute-start(bf16[128,1024]{0,1:T(8,128)(2,1)S(1)} %get-tuple-element.619), channel_id=1, source_target_pairs={{0,4},{4,8},{8,12},{12,16},{16,20},{20,24},{24,28},{1,5},{5,9},{9,... | collective-permute-start | bytes 786440 | tf_op jit(solution)/shard_map/while/body/eval_jaxpr/ppermute | solution.py:12
  30.2 9.4 %collective-permute-start = (bf16[128,1024]{0,1:T(8,128)(2,1)S(1)}, bf16[128,1024]{0,1:T(8,128)(2,1)S(1)}, u32[]{:S(2)}, u32[]{:S(2)}) collective-permute-start(bf16[128,1024]{0,1:T(8,128)(2,1)S(1)} %get-tuple-element.618), channel_id=1, source_target_pairs={{0,4},{4,8},{8,12},{12,16},{16,20},{20,24},{24,28},{1,5},{5,9},{9,... | collective-permute-start | bytes 786440 | tf_op jit(solution)/shard_map/while/body/eval_jaxpr/ppermute | solution.py:12
  35.2 5.5 %collective-permute-start.1 = (bf16[128,1024]{0,1:T(8,128)(2,1)S(1)}, bf16[128,1024]{0,1:T(8,128)(2,1)S(1)}, u32[]{:S(2)}, u32[]{:S(2)}) collective-permute-start(bf16[128,1024]{0,1:T(8,128)(2,1)S(1)} %get-tuple-element.619), channel_id=1, source_target_pairs={{0,4},{4,8},{8,12},{12,16},{16,20},{20,24},{24,28},{1,5},{5,9},{9,... | collective-permute-start | bytes 786440 | tf_op jit(solution)/shard_map/while/body/eval_jaxpr/ppermute | solution.py:12
  41.8 9.4 %collective-permute-start = (bf16[128,1024]{0,1:T(8,128)(2,1)S(1)}, bf16[128,1024]{0,1:T(8,128)(2,1)S(1)}, u32[]{:S(2)}, u32[]{:S(2)}) collective-permute-start(bf16[128,1024]{0,1:T(8,128)(2,1)S(1)} %get-tuple-element.618), channel_id=1, source_target_pairs={{0,4},{4,8},{8,12},{12,16},{16,20},{20,24},{24,28},{1,5},{5,9},{9,... | collective-permute-start | bytes 786440 | tf_op jit(solution)/shard_map/while/body/eval_jaxpr/ppermute | solution.py:12
  46.8 5.5 %collective-permute-start.1 = (bf16[128,1024]{0,1:T(8,128)(2,1)S(1)}, bf16[128,1024]{0,1:T(8,128)(2,1)S(1)}, u32[]{:S(2)}, u32[]{:S(2)}) collective-permute-start(bf16[128,1024]{0,1:T(8,128)(2,1)S(1)} %get-tuple-element.619), channel_id=1, source_target_pairs={{0,4},{4,8},{8,12},{12,16},{16,20},{20,24},{24,28},{1,5},{5,9},{9,... | collective-permute-start | bytes 786440 | tf_op jit(solution)/shard_map/while/body/eval_jaxpr/ppermute | solution.py:12
  53.5 9.4 %collective-permute-start = (bf16[128,1024]{0,1:T(8,128)(2,1)S(1)}, bf16[128,1024]{0,1:T(8,128)(2,1)S(1)}, u32[]{:S(2)}, u32[]{:S(2)}) collective-permute-start(bf16[128,1024]{0,1:T(8,128)(2,1)S(1)} %get-tuple-element.618), channel_id=1, source_target_pairs={{0,4},{4,8},{8,12},{12,16},{16,20},{20,24},{24,28},{1,5},{5,9},{9,... | collective-permute-start | bytes 786440 | tf_op jit(solution)/shard_map/while/body/eval_jaxpr/ppermute | solution.py:12
  58.4 5.5 %collective-permute-start.1 = (bf16[128,1024]{0,1:T(8,128)(2,1)S(1)}, bf16[128,1024]{0,1:T(8,128)(2,1)S(1)}, u32[]{:S(2)}, u32[]{:S(2)}) collective-permute-start(bf16[128,1024]{0,1:T(8,128)(2,1)S(1)} %get-tuple-element.619), channel_id=1, source_target_pairs={{0,4},{4,8},{8,12},{12,16},{16,20},{20,24},{24,28},{1,5},{5,9},{9,... | collective-permute-start | bytes 786440 | tf_op jit(solution)/shard_map/while/body/eval_jaxpr/ppermute | solution.py:12
  65.1 9.4 %collective-permute-start = (bf16[128,1024]{0,1:T(8,128)(2,1)S(1)}, bf16[128,1024]{0,1:T(8,128)(2,1)S(1)}, u32[]{:S(2)}, u32[]{:S(2)}) collective-permute-start(bf16[128,1024]{0,1:T(8,128)(2,1)S(1)} %get-tuple-element.618), channel_id=1, source_target_pairs={{0,4},{4,8},{8,12},{12,16},{16,20},{20,24},{24,28},{1,5},{5,9},{9,... | collective-permute-start | bytes 786440 | tf_op jit(solution)/shard_map/while/body/eval_jaxpr/ppermute | solution.py:12
  70.1 5.5 %collective-permute-start.1 = (bf16[128,1024]{0,1:T(8,128)(2,1)S(1)}, bf16[128,1024]{0,1:T(8,128)(2,1)S(1)}, u32[]{:S(2)}, u32[]{:S(2)}) collective-permute-start(bf16[128,1024]{0,1:T(8,128)(2,1)S(1)} %get-tuple-element.619), channel_id=1, source_target_pairs={{0,4},{4,8},{8,12},{12,16},{16,20},{20,24},{24,28},{1,5},{5,9},{9,... | collective-permute-start | bytes 786440 | tf_op jit(solution)/shard_map/while/body/eval_jaxpr/ppermute | solution.py:12
  76.7 9.4 %collective-permute-start = (bf16[128,1024]{0,1:T(8,128)(2,1)S(1)}, bf16[128,1024]{0,1:T(8,128)(2,1)S(1)}, u32[]{:S(2)}, u32[]{:S(2)}) collective-permute-start(bf16[128,1024]{0,1:T(8,128)(2,1)S(1)} %get-tuple-element.618), channel_id=1, source_target_pairs={{0,4},{4,8},{8,12},{12,16},{16,20},{20,24},{24,28},{1,5},{5,9},{9,... | collective-permute-start | bytes 786440 | tf_op jit(solution)/shard_map/while/body/eval_jaxpr/ppermute | solution.py:12
  81.7 5.5 %collective-permute-start.1 = (bf16[128,1024]{0,1:T(8,128)(2,1)S(1)}, bf16[128,1024]{0,1:T(8,128)(2,1)S(1)}, u32[]{:S(2)}, u32[]{:S(2)}) collective-permute-start(bf16[128,1024]{0,1:T(8,128)(2,1)S(1)} %get-tuple-element.619), channel_id=1, source_target_pairs={{0,4},{4,8},{8,12},{12,16},{16,20},{20,24},{24,28},{1,5},{5,9},{9,... | collective-permute-start | bytes 786440 | tf_op jit(solution)/shard_map/while/body/eval_jaxpr/ppermute | solution.py:12
  88.3 1.0 copy-start.1
  88.3 1.1 copy-start.3
  89.8 7.6 %collective-permute-start.2 = (bf16[128,1024]{0,1:T(8,128)(2,1)S(1)}, bf16[128,1024]{0,1:T(8,128)(2,1)S(1)}, u32[]{:S(2)}, u32[]{:S(2)}) collective-permute-start(bf16[128,1024]{0,1:T(8,128)(2,1)S(1)} %get-tuple-element.650), channel_id=1, source_target_pairs={{4,0},{8,4},{12,8},{16,12},{20,16},{24,20},{28,24},{5,1},{9,5},{13... | collective-permute-start | bytes 786440 | tf_op jit(solution)/shard_map/while/body/eval_jaxpr/ppermute | solution.py:12
  91.1 6.2 %collective-permute-start.3 = (bf16[128,4,8]{0,2,1:T(8,128)(2,1)S(1)}, bf16[128,4,8]{0,2,1:T(8,128)(2,1)S(1)}, u32[]{:S(2)}, u32[]{:S(2)}) collective-permute-start(bf16[128,4,8]{0,2,1:T(8,128)(2,1)S(1)} %get-tuple-element.652), channel_id=1, source_target_pairs={{4,0},{8,4},{12,8},{16,12},{20,16},{24,20},{28,24},{5,1},{9,5},{13... | collective-permute-start | bytes 24584 | tf_op jit(solution)/shard_map/while/body/eval_jaxpr/ppermute | solution.py:12
  92.4 7.2 %collective-permute-start.4 = (bf16[128,1024]{0,1:T(8,128)(2,1)S(1)}, bf16[128,1024]{0,1:T(8,128)(2,1)S(1)}, u32[]{:S(2)}, u32[]{:S(2)}) collective-permute-start(bf16[128,1024]{0,1:T(8,128)(2,1)S(1)} %get-tuple-element.651), channel_id=1, source_target_pairs={{4,0},{8,4},{12,8},{16,12},{20,16},{24,20},{28,24},{5,1},{9,5},{13... | collective-permute-start | bytes 786440 | tf_op jit(solution)/shard_map/while/body/eval_jaxpr/ppermute | solution.py:12
  100.6 10.0 %collective-permute-start.2 = (bf16[128,1024]{0,1:T(8,128)(2,1)S(1)}, bf16[128,1024]{0,1:T(8,128)(2,1)S(1)}, u32[]{:S(2)}, u32[]{:S(2)}) collective-permute-start(bf16[128,1024]{0,1:T(8,128)(2,1)S(1)} %get-tuple-element.650), channel_id=1, source_target_pairs={{4,0},{8,4},{12,8},{16,12},{20,16},{24,20},{28,24},{5,1},{9,5},{13... | collective-permute-start | bytes 786440 | tf_op jit(solution)/shard_map/while/body/eval_jaxpr/ppermute | solution.py:12
  101.9 8.7 %collective-permute-start.3 = (bf16[128,4,8]{0,2,1:T(8,128)(2,1)S(1)}, bf16[128,4,8]{0,2,1:T(8,128)(2,1)S(1)}, u32[]{:S(2)}, u32[]{:S(2)}) collective-permute-start(bf16[128,4,8]{0,2,1:T(8,128)(2,1)S(1)} %get-tuple-element.652), channel_id=1, source_target_pairs={{4,0},{8,4},{12,8},{16,12},{20,16},{24,20},{28,24},{5,1},{9,5},{13... | collective-permute-start | bytes 24584 | tf_op jit(solution)/shard_map/while/body/eval_jaxpr/ppermute | solution.py:12
  103.2 9.7 %collective-permute-start.4 = (bf16[128,1024]{0,1:T(8,128)(2,1)S(1)}, bf16[128,1024]{0,1:T(8,128)(2,1)S(1)}, u32[]{:S(2)}, u32[]{:S(2)}) collective-permute-start(bf16[128,1024]{0,1:T(8,128)(2,1)S(1)} %get-tuple-element.651), channel_id=1, source_target_pairs={{4,0},{8,4},{12,8},{16,12},{20,16},{24,20},{28,24},{5,1},{9,5},{13... | collective-permute-start | bytes 786440 | tf_op jit(solution)/shard_map/while/body/eval_jaxpr/ppermute | solution.py:12
  113.9 9.3 %collective-permute-start.2 = (bf16[128,1024]{0,1:T(8,128)(2,1)S(1)}, bf16[128,1024]{0,1:T(8,128)(2,1)S(1)}, u32[]{:S(2)}, u32[]{:S(2)}) collective-permute-start(bf16[128,1024]{0,1:T(8,128)(2,1)S(1)} %get-tuple-element.650), channel_id=1, source_target_pairs={{4,0},{8,4},{12,8},{16,12},{20,16},{24,20},{28,24},{5,1},{9,5},{13... | collective-permute-start | bytes 786440 | tf_op jit(solution)/shard_map/while/body/eval_jaxpr/ppermute | solution.py:12
  115.2 8.0 %collective-permute-start.3 = (bf16[128,4,8]{0,2,1:T(8,128)(2,1)S(1)}, bf16[128,4,8]{0,2,1:T(8,128)(2,1)S(1)}, u32[]{:S(2)}, u32[]{:S(2)}) collective-permute-start(bf16[128,4,8]{0,2,1:T(8,128)(2,1)S(1)} %get-tuple-element.652), channel_id=1, source_target_pairs={{4,0},{8,4},{12,8},{16,12},{20,16},{24,20},{28,24},{5,1},{9,5},{13... | collective-permute-start | bytes 24584 | tf_op jit(solution)/shard_map/while/body/eval_jaxpr/ppermute | solution.py:12
  116.5 9.0 %collective-permute-start.4 = (bf16[128,1024]{0,1:T(8,128)(2,1)S(1)}, bf16[128,1024]{0,1:T(8,128)(2,1)S(1)}, u32[]{:S(2)}, u32[]{:S(2)}) collective-permute-start(bf16[128,1024]{0,1:T(8,128)(2,1)S(1)} %get-tuple-element.651), channel_id=1, source_target_pairs={{4,0},{8,4},{12,8},{16,12},{20,16},{24,20},{28,24},{5,1},{9,5},{13... | collective-permute-start | bytes 786440 | tf_op jit(solution)/shard_map/while/body/eval_jaxpr/ppermute | solution.py:12
  126.5 9.3 %collective-permute-start.2 = (bf16[128,1024]{0,1:T(8,128)(2,1)S(1)}, bf16[128,1024]{0,1:T(8,128)(2,1)S(1)}, u32[]{:S(2)}, u32[]{:S(2)}) collective-permute-start(bf16[128,1024]{0,1:T(8,128)(2,1)S(1)} %get-tuple-element.650), channel_id=1, source_target_pairs={{4,0},{8,4},{12,8},{16,12},{20,16},{24,20},{28,24},{5,1},{9,5},{13... | collective-permute-start | bytes 786440 | tf_op jit(solution)/shard_map/while/body/eval_jaxpr/ppermute | solution.py:12
  127.8 8.0 %collective-permute-start.3 = (bf16[128,4,8]{0,2,1:T(8,128)(2,1)S(1)}, bf16[128,4,8]{0,2,1:T(8,128)(2,1)S(1)}, u32[]{:S(2)}, u32[]{:S(2)}) collective-permute-start(bf16[128,4,8]{0,2,1:T(8,128)(2,1)S(1)} %get-tuple-element.652), channel_id=1, source_target_pairs={{4,0},{8,4},{12,8},{16,12},{20,16},{24,20},{28,24},{5,1},{9,5},{13... | collective-permute-start | bytes 24584 | tf_op jit(solution)/shard_map/while/body/eval_jaxpr/ppermute | solution.py:12
  129.1 9.0 %collective-permute-start.4 = (bf16[128,1024]{0,1:T(8,128)(2,1)S(1)}, bf16[128,1024]{0,1:T(8,128)(2,1)S(1)}, u32[]{:S(2)}, u32[]{:S(2)}) collective-permute-start(bf16[128,1024]{0,1:T(8,128)(2,1)S(1)} %get-tuple-element.651), channel_id=1, source_target_pairs={{4,0},{8,4},{12,8},{16,12},{20,16},{24,20},{28,24},{5,1},{9,5},{13... | collective-permute-start | bytes 786440 | tf_op jit(solution)/shard_map/while/body/eval_jaxpr/ppermute | solution.py:12
  139.1 9.3 %collective-permute-start.2 = (bf16[128,1024]{0,1:T(8,128)(2,1)S(1)}, bf16[128,1024]{0,1:T(8,128)(2,1)S(1)}, u32[]{:S(2)}, u32[]{:S(2)}) collective-permute-start(bf16[128,1024]{0,1:T(8,128)(2,1)S(1)} %get-tuple-element.650), channel_id=1, source_target_pairs={{4,0},{8,4},{12,8},{16,12},{20,16},{24,20},{28,24},{5,1},{9,5},{13... | collective-permute-start | bytes 786440 | tf_op jit(solution)/shard_map/while/body/eval_jaxpr/ppermute | solution.py:12
  140.4 8.0 %collective-permute-start.3 = (bf16[128,4,8]{0,2,1:T(8,128)(2,1)S(1)}, bf16[128,4,8]{0,2,1:T(8,128)(2,1)S(1)}, u32[]{:S(2)}, u32[]{:S(2)}) collective-permute-start(bf16[128,4,8]{0,2,1:T(8,128)(2,1)S(1)} %get-tuple-element.652), channel_id=1, source_target_pairs={{4,0},{8,4},{12,8},{16,12},{20,16},{24,20},{28,24},{5,1},{9,5},{13... | collective-permute-start | bytes 24584 | tf_op jit(solution)/shard_map/while/body/eval_jaxpr/ppermute | solution.py:12
  141.7 8.9 %collective-permute-start.4 = (bf16[128,1024]{0,1:T(8,128)(2,1)S(1)}, bf16[128,1024]{0,1:T(8,128)(2,1)S(1)}, u32[]{:S(2)}, u32[]{:S(2)}) collective-permute-start(bf16[128,1024]{0,1:T(8,128)(2,1)S(1)} %get-tuple-element.651), channel_id=1, source_target_pairs={{4,0},{8,4},{12,8},{16,12},{20,16},{24,20},{28,24},{5,1},{9,5},{13... | collective-permute-start | bytes 786440 | tf_op jit(solution)/shard_map/while/body/eval_jaxpr/ppermute | solution.py:12
  151.6 9.3 %collective-permute-start.2 = (bf16[128,1024]{0,1:T(8,128)(2,1)S(1)}, bf16[128,1024]{0,1:T(8,128)(2,1)S(1)}, u32[]{:S(2)}, u32[]{:S(2)}) collective-permute-start(bf16[128,1024]{0,1:T(8,128)(2,1)S(1)} %get-tuple-element.650), channel_id=1, source_target_pairs={{4,0},{8,4},{12,8},{16,12},{20,16},{24,20},{28,24},{5,1},{9,5},{13... | collective-permute-start | bytes 786440 | tf_op jit(solution)/shard_map/while/body/eval_jaxpr/ppermute | solution.py:12
  152.9 8.0 %collective-permute-start.3 = (bf16[128,4,8]{0,2,1:T(8,128)(2,1)S(1)}, bf16[128,4,8]{0,2,1:T(8,128)(2,1)S(1)}, u32[]{:S(2)}, u32[]{:S(2)}) collective-permute-start(bf16[128,4,8]{0,2,1:T(8,128)(2,1)S(1)} %get-tuple-element.652), channel_id=1, source_target_pairs={{4,0},{8,4},{12,8},{16,12},{20,16},{24,20},{28,24},{5,1},{9,5},{13... | collective-permute-start | bytes 24584 | tf_op jit(solution)/shard_map/while/body/eval_jaxpr/ppermute | solution.py:12
  154.2 8.9 %collective-permute-start.4 = (bf16[128,1024]{0,1:T(8,128)(2,1)S(1)}, bf16[128,1024]{0,1:T(8,128)(2,1)S(1)}, u32[]{:S(2)}, u32[]{:S(2)}) collective-permute-start(bf16[128,1024]{0,1:T(8,128)(2,1)S(1)} %get-tuple-element.651), channel_id=1, source_target_pairs={{4,0},{8,4},{12,8},{16,12},{20,16},{24,20},{28,24},{5,1},{9,5},{13... | collective-permute-start | bytes 786440 | tf_op jit(solution)/shard_map/while/body/eval_jaxpr/ppermute | solution.py:12
  164.2 9.3 %collective-permute-start.2 = (bf16[128,1024]{0,1:T(8,128)(2,1)S(1)}, bf16[128,1024]{0,1:T(8,128)(2,1)S(1)}, u32[]{:S(2)}, u32[]{:S(2)}) collective-permute-start(bf16[128,1024]{0,1:T(8,128)(2,1)S(1)} %get-tuple-element.650), channel_id=1, source_target_pairs={{4,0},{8,4},{12,8},{16,12},{20,16},{24,20},{28,24},{5,1},{9,5},{13... | collective-permute-start | bytes 786440 | tf_op jit(solution)/shard_map/while/body/eval_jaxpr/ppermute | solution.py:12
  165.5 8.0 %collective-permute-start.3 = (bf16[128,4,8]{0,2,1:T(8,128)(2,1)S(1)}, bf16[128,4,8]{0,2,1:T(8,128)(2,1)S(1)}, u32[]{:S(2)}, u32[]{:S(2)}) collective-permute-start(bf16[128,4,8]{0,2,1:T(8,128)(2,1)S(1)} %get-tuple-element.652), channel_id=1, source_target_pairs={{4,0},{8,4},{12,8},{16,12},{20,16},{24,20},{28,24},{5,1},{9,5},{13... | collective-permute-start | bytes 24584 | tf_op jit(solution)/shard_map/while/body/eval_jaxpr/ppermute | solution.py:12
  166.8 8.9 %collective-permute-start.4 = (bf16[128,1024]{0,1:T(8,128)(2,1)S(1)}, bf16[128,1024]{0,1:T(8,128)(2,1)S(1)}, u32[]{:S(2)}, u32[]{:S(2)}) collective-permute-start(bf16[128,1024]{0,1:T(8,128)(2,1)S(1)} %get-tuple-element.651), channel_id=1, source_target_pairs={{4,0},{8,4},{12,8},{16,12},{20,16},{24,20},{28,24},{5,1},{9,5},{13... | collective-permute-start | bytes 786440 | tf_op jit(solution)/shard_map/while/body/eval_jaxpr/ppermute | solution.py:12
  176.8 1.7 copy-start.11
  181.5 11.6 %copy-start.4 = (bf16[128,2048]{1,0:T(8,128)(2,1)S(1)}, bf16[128,2048]{1,0:T(8,128)(2,1)}, u32[]{:S(2)}) copy-start(bf16[128,2048]{1,0:T(8,128)(2,1)} %param.21) | copy-start | bytes 1572868
  181.6 11.6 %copy-start.5 = (bf16[128,2048]{1,0:T(8,128)(2,1)S(1)}, bf16[128,2048]{1,0:T(8,128)(2,1)}, u32[]{:S(2)}) copy-start(bf16[128,2048]{1,0:T(8,128)(2,1)} %param.22) | copy-start | bytes 1572868
where the time goes:
time: 254 us; the launch traced here: 253 us
  starting transfers between devices  92.3 us (36%)
  waiting for transfers between devices  54.4 us (21%)
  blocking collectives  44.9 us (18%)
  matrix products  43.7 us (17%)
  other arithmetic  8.44 us (3%)
  local copies, waits for them, and re-layouts  6.71 us (3%)
    ppermute x36, starting transfers between devices, from_behind(): lax.ppermute(value, axis, [(source, source + steps) for source in range(l...  92.3 us
    ppermute x36, waiting for transfers between devices, from_behind(): lax.ppermute(value, axis, [(source, source + steps) for source in range(l...  54.4 us
    psum x1, blocking collectives, local(): filter_total = lax.psum(local_terms, ('seq', 'tp'))  44.9 us
    conv_general_dilated x1, matrix products, local(): lax.conv_general_dilated(padded[None], mixed[:, None, :], (1,), 'VALID',...  11.7 us
    conv_general_dilated x1, matrix products, local(): lax.conv_general_dilated(padded[None], taps[:, None, :], (1,), 'VALID', d...  11.6 us
    dot_general x8, matrix products, query_tile(): jnp.einsum('hqk,khd->qhd', weights * (dprob - delta_heads[:, :, None]), k...  5.68 us
  transfers between devices with their start and end apart: 36, of which 21 were waited for; matrix products, arithmetic and copies ran while one was open for 11% of the time, Pallas kernels for 0%

commit v1 on v0

--- a/solution.py
+++ b/solution.py
@@ -174,7 +174,8 @@
     grad_feat_k = (dw * feat_v.astype(jnp.float32)).astype(jnp.bfloat16)
     grad_feat_v = (dw * feat_k.astype(jnp.float32)).astype(jnp.bfloat16)
     local_terms = jnp.sum(local_terms.reshape(span_taps, channels // groups, groups), axis=1).T
-    filter_total = lax.psum(local_terms, ("seq", "tp"))
+    blocks = lax.all_gather(local_terms, ("seq", "tp"))
+    filter_total = jnp.sum(blocks, axis=0)
     count_all = rows * shards * channels * lax.axis_size("tp") / groups
     grad_filters = filter_total * (1.0 / count_all**0.5)
     return (grad_q, grad_k, grad_v, grad_gate, grad_feat_k, grad_feat_v, grad_filters)

time: 254 us -> 239 us (0.941)
  the two profiles are of different devices: /device:TPU:0 before, /device:TPU:23 now
where the time goes in v1:
time: 239 us; the launch traced here: 238 us
  starting transfers between devices  89.9 us (38%)
  waiting for transfers between devices  63.5 us (27%)
  matrix products  44.1 us (18%)
  local copies, waits for them, and re-layouts  14.4 us (6%)
  between operations  14.4 us (6%)
  other arithmetic  10.4 us (4%)
    ppermute x36, starting transfers between devices, from_behind(): lax.ppermute(value, axis, [(source, source + steps) for source in range(l...  89.9 us
    ppermute x36, waiting for transfers between devices, from_behind(): lax.ppermute(value, axis, [(source, source + steps) for source in range(l...  63.5 us
    conv_general_dilated x1, matrix products, local(): lax.conv_general_dilated(padded[None], mixed[:, None, :], (1,), 'VALID',...  12.2 us
    conv_general_dilated x1, matrix products, local(): lax.conv_general_dilated(padded[None], taps[:, None, :], (1,), 'VALID', d...  11.4 us
    dot_general x8, matrix products, query_tile(): jnp.einsum('hqk,khd->qhd', weights * (dprob - delta_heads[:, :, None]), k...  5.68 us
    while x42, local copies, waits for them, and re-layouts  5.36 us
  transfers between devices with their start and end apart: 37, of which 28 were waited for; matrix products, arithmetic and copies ran while one was open for 14% of the time, Pallas kernels for 0%

profile of v1, /device:TPU:23, one launch (start us, length us, event | category | flops | bytes accessed | tf_op | source)
XLA Modules:
  0.0 237.8 jit_solution(14766460130722222464)
XLA Ops:
  7.2 2.7 %fusion.19 = (bf16[128,2048]{1,0:T(8,128)(2,1)}, bf16[128,2048]{1,0:T(8,128)(2,1)}) fusion(bf16[128,2048]{1,0:T(8,128)(2,1)} %param.24, bf16[128,2048]{1,0:T(8,128)(2,1)} %param.20, bf16[128,2048]{1,0:T(8,128)(2,1)} %param.23), kind=kLoop, calls=%fused_computation.41 | loop fusion | flops 1835008 | bytes 2621440 | tf_op jit(solution)/shard_map/convert_element_type | solution.py:149
  9.9 2.7 %collective-permute-start.5 = (bf16[127,2048]{1,0:T(8,128)(2,1)}, bf16[127,2048]{1,0:T(8,128)(2,1)}, u32[]{:S(2)}, u32[]{:S(2)}) collective-permute-start(bf16[127,2048]{1,0:T(8,128)(2,1)} %bitcast.111), channel_id=1, source_target_pairs={{4,0},{8,4},{12,8},{16,12},{20,16},{24,20},{28,24},{5,1},{9,5},{13... | collective-permute-start | bytes 1560584 | tf_op jit(solution)/shard_map/ppermute | solution.py:12
  16.5 80.5 %while.42 = (s32[]{:T(128)}, f32[8,128]{1,0:T(8,128)S(1)}, f32[8,128]{1,0:T(8,128)S(1)}, f32[128,8,128]{2,0,1:T(8,128)S(1)}, bf16[128,1024]{0,1:T(8,128)(2,1)S(1...) while((s32[]{:T(128)}, f32[8,128]{1,0:T(8,128)S(1)}, ...), condition=%wide.region_6.7_spmd, body=%wide.region_3.6_spmd.sunk | while | flops 270011392 | bytes 8196297 | solution.py:92
  16.5 3.1 %collective-permute-start = (bf16[128,1024]{0,1:T(8,128)(2,1)S(1)}, bf16[128,1024]{0,1:T(8,128)(2,1)S(1)}, u32[]{:S(2)}, u32[]{:S(2)}) collective-permute-start(bf16[128,1024]{0,1:T(8,128)(2,1)S(1)} %get-tuple-element.618), channel_id=1, source_target_pairs={{0,4},{4,8},{8,12},{12,16},{16,20},{20,24},{24,28},{1,5},{5,9},{9,... | collective-permute-start | bytes 786440 | tf_op jit(solution)/shard_map/while/body/eval_jaxpr/ppermute | solution.py:12
  19.7 3.2 %collective-permute-start.1 = (bf16[128,1024]{0,1:T(8,128)(2,1)S(1)}, bf16[128,1024]{0,1:T(8,128)(2,1)S(1)}, u32[]{:S(2)}, u32[]{:S(2)}) collective-permute-start(bf16[128,1024]{0,1:T(8,128)(2,1)S(1)} %get-tuple-element.619), channel_id=1, source_target_pairs={{0,4},{4,8},{8,12},{12,16},{16,20},{20,24},{24,28},{1,5},{5,9},{9,... | collective-permute-start | bytes 786440 | tf_op jit(solution)/shard_map/while/body/eval_jaxpr/ppermute | solution.py:12
  23.4 2.7 %collective-permute-done.1 = bf16[128,1024]{0,1:T(8,128)(2,1)S(1)} collective-permute-done((bf16[128,1024]{0,1:T(8,128)(2,1)S(1)}, bf16[128,1024]{0,1:T(8,128)(2,1)S(1)}, u32[]{:S(2)}, u32[]{:S(2)}) %collective-permute-start.1) | collective-permute-done | bytes 262176 | tf_op jit(solution)/shard_map/while/body/eval_jaxpr/ppermute | solution.py:12
  27.3 4.4 %collective-permute-start = (bf16[128,1024]{0,1:T(8,128)(2,1)S(1)}, bf16[128,1024]{0,1:T(8,128)(2,1)S(1)}, u32[]{:S(2)}, u32[]{:S(2)}) collective-permute-start(bf16[128,1024]{0,1:T(8,128)(2,1)S(1)} %get-tuple-element.618), channel_id=1, source_target_pairs={{0,4},{4,8},{8,12},{12,16},{16,20},{20,24},{24,28},{1,5},{5,9},{9,... | collective-permute-start | bytes 786440 | tf_op jit(solution)/shard_map/while/body/eval_jaxpr/ppermute | solution.py:12
  31.7 1.9 collective-permute-start.1
  35.5 2.3 collective-permute-done.1
  38.9 4.4 %collective-permute-start = (bf16[128,1024]{0,1:T(8,128)(2,1)S(1)}, bf16[128,1024]{0,1:T(8,128)(2,1)S(1)}, u32[]{:S(2)}, u32[]{:S(2)}) collective-permute-start(bf16[128,1024]{0,1:T(8,128)(2,1)S(1)} %get-tuple-element.618), channel_id=1, source_target_pairs={{0,4},{4,8},{8,12},{12,16},{16,20},{20,24},{24,28},{1,5},{5,9},{9,... | collective-permute-start | bytes 786440 | tf_op jit(solution)/shard_map/while/body/eval_jaxpr/ppermute | solution.py:12
  43.3 1.9 collective-permute-start.1
  47.1 2.3 collective-permute-done.1
  50.6 4.4 %collective-permute-start = (bf16[128,1024]{0,1:T(8,128)(2,1)S(1)}, bf16[128,1024]{0,1:T(8,128)(2,1)S(1)}, u32[]{:S(2)}, u32[]{:S(2)}) collective-permute-start(bf16[128,1024]{0,1:T(8,128)(2,1)S(1)} %get-tuple-element.618), channel_id=1, source_target_pairs={{0,4},{4,8},{8,12},{12,16},{16,20},{20,24},{24,28},{1,5},{5,9},{9,... | collective-permute-start | bytes 786440 | tf_op jit(solution)/shard_map/while/body/eval_jaxpr/ppermute | solution.py:12
  55.0 1.9 collective-permute-start.1
  58.8 2.3 collective-permute-done.1
  62.2 4.4 %collective-permute-start = (bf16[128,1024]{0,1:T(8,128)(2,1)S(1)}, bf16[128,1024]{0,1:T(8,128)(2,1)S(1)}, u32[]{:S(2)}, u32[]{:S(2)}) collective-permute-start(bf16[128,1024]{0,1:T(8,128)(2,1)S(1)} %get-tuple-element.618), channel_id=1, source_target_pairs={{0,4},{4,8},{8,12},{12,16},{16,20},{20,24},{24,28},{1,5},{5,9},{9,... | collective-permute-start | bytes 786440 | tf_op jit(solution)/shard_map/while/body/eval_jaxpr/ppermute | solution.py:12
  66.6 1.9 collective-permute-start.1
  70.4 2.3 collective-permute-done.1
  73.8 4.4 %collective-permute-start = (bf16[128,1024]{0,1:T(8,128)(2,1)S(1)}, bf16[128,1024]{0,1:T(8,128)(2,1)S(1)}, u32[]{:S(2)}, u32[]{:S(2)}) collective-permute-start(bf16[128,1024]{0,1:T(8,128)(2,1)S(1)} %get-tuple-element.618), channel_id=1, source_target_pairs={{0,4},{4,8},{8,12},{12,16},{16,20},{20,24},{24,28},{1,5},{5,9},{9,... | collective-permute-start | bytes 786440 | tf_op jit(solution)/shard_map/while/body/eval_jaxpr/ppermute | solution.py:12
  78.2 1.9 collective-permute-start.1
  82.0 2.3 collective-permute-done.1
  85.4 4.4 %collective-permute-start = (bf16[128,1024]{0,1:T(8,128)(2,1)S(1)}, bf16[128,1024]{0,1:T(8,128)(2,1)S(1)}, u32[]{:S(2)}, u32[]{:S(2)}) collective-permute-start(bf16[128,1024]{0,1:T(8,128)(2,1)S(1)} %get-tuple-element.618), channel_id=1, source_target_pairs={{0,4},{4,8},{8,12},{12,16},{16,20},{20,24},{24,28},{1,5},{5,9},{9,... | collective-permute-start | bytes 786440 | tf_op jit(solution)/shard_map/while/body/eval_jaxpr/ppermute | solution.py:12
  89.8 1.9 collective-permute-start.1
  93.6 2.3 collective-permute-done.1
  97.2 1.9 copy.197
  102.1 11.4 %fusion.15 = f32[1,128,2048]{2,0,1:T(1,128)S(1)} fusion(f32[128,1,2048]{2,1,0:T(1,128)S(1)} %copy-done.4, bf16[1,255,2048]{2,1,0:T(8,128)(2,1)S(1)} %maximum_bitcast_fusion), kind=kOutput, calls=%fused_computation.28 | convolution fusion | flops 402653184 | bytes 3141632 | tf_op jit(solution)/shard_map/conv_general_dilated | solution.py:156
  113.5 1.6 fusion.21
  115.1 12.2 %fusion.13 = f32[1,128,2048]{2,0,1:T(1,128)} fusion(bf16[1,255,2048]{2,1,0:T(8,128)(2,1)S(1)} %maximum_bitcast_fusion, f32[128,1,2048]{2,0,1:T(8,128)S(1)} %get-tuple-element.462), kind=kOutput, calls=%fused_computation.26 | convolution fusion | flops 402653184 | bytes 3141632 | tf_op jit(solution)/shard_map/conv_general_dilated | solution.py:165
  127.3 2.3 copy.200
  130.4 96.1 %while.43 = (s32[]{:T(128)}, f32[128,8,128]{2,0,1:T(8,128)S(1)}, f32[128,8,128]{2,0,1:T(8,128)S(1)}, bf16[128,1024]{0,1:T(8,128)(2,1)}, bf16[128,1024]{0,1:T(8,1...) while((s32[]{:T(128)}, f32[128,8,128]{2,0,1:T(8,128)S(1)}, ...), condition=%wide.region_8.9_spmd, body=%wide.region_7.8_spmd.sunk | while | flops 135403520 | bytes 8462587 | solution.py:141
  130.4 2.8 %collective-permute-start.2 = (bf16[128,1024]{0,1:T(8,128)(2,1)}, bf16[128,1024]{0,1:T(8,128)(2,1)S(1)}, u32[]{:S(2)}, u32[]{:S(2)}) collective-permute-start(bf16[128,1024]{0,1:T(8,128)(2,1)} %get-tuple-element.650), channel_id=1, source_target_pairs={{4,0},{8,4},{12,8},{16,12},{20,16},{24,20},{28,24},{5,1},{9,5},{13... | collective-permute-start | bytes 786440 | tf_op jit(solution)/shard_map/while/body/eval_jaxpr/ppermute | solution.py:12
  133.2 1.9 collective-permute-start.3
  135.1 2.5 %collective-permute-start.4 = (bf16[128,1024]{0,1:T(8,128)(2,1)S(1)}, bf16[128,1024]{0,1:T(8,128)(2,1)S(1)}, u32[]{:S(2)}, u32[]{:S(2)}) collective-permute-start(bf16[128,1024]{0,1:T(8,128)(2,1)S(1)} %get-tuple-element.651), channel_id=1, source_target_pairs={{4,0},{8,4},{12,8},{16,12},{20,16},{24,20},{28,24},{5,1},{9,5},{13... | collective-permute-start | bytes 786440 | tf_op jit(solution)/shard_map/while/body/eval_jaxpr/ppermute | solution.py:12
  139.5 3.7 %collective-permute-done.4 = bf16[128,1024]{0,1:T(8,128)(2,1)S(1)} collective-permute-done((bf16[128,1024]{0,1:T(8,128)(2,1)S(1)}, bf16[128,1024]{0,1:T(8,128)(2,1)S(1)}, u32[]{:S(2)}, u32[]{:S(2)}) %collective-permute-start.4) | collective-permute-done | bytes 262176 | tf_op jit(solution)/shard_map/while/body/eval_jaxpr/ppermute | solution.py:12
  144.9 1.9 collective-permute-start.2
  146.8 2.1 collective-permute-start.3
  148.9 1.9 collective-permute-start.4
  150.8 2.1 collective-permute-done.3
  153.3 3.3 %collective-permute-done.4 = bf16[128,1024]{0,1:T(8,128)(2,1)S(1)} collective-permute-done((bf16[128,1024]{0,1:T(8,128)(2,1)S(1)}, bf16[128,1024]{0,1:T(8,128)(2,1)S(1)}, u32[]{:S(2)}, u32[]{:S(2)}) %collective-permute-start.4) | collective-permute-done | bytes 262176 | tf_op jit(solution)/shard_map/while/body/eval_jaxpr/ppermute | solution.py:12
  158.2 1.9 collective-permute-start.2
  160.1 1.9 collective-permute-start.3
  162.1 1.9 collective-permute-start.4
  164.0 3.0 %collective-permute-done.3 = bf16[128,4,8]{0,2,1:T(8,128)(2,1)S(1)} collective-permute-done((bf16[128,4,8]{0,2,1:T(8,128)(2,1)S(1)}, bf16[128,4,8]{0,2,1:T(8,128)(2,1)S(1)}, u32[]{:S(2)}, u32[]{:S(2)}) %collective-permute-start.3) | collective-permute-done | bytes 8224 | tf_op jit(solution)/shard_map/while/body/eval_jaxpr/ppermute | solution.py:12
  167.4 2.4 collective-permute-done.4
  171.4 1.9 collective-permute-start.2
  173.4 2.1 collective-permute-start.3
  175.4 1.9 collective-permute-start.4
  177.4 3.5 %collective-permute-done.3 = bf16[128,4,8]{0,2,1:T(8,128)(2,1)S(1)} collective-permute-done((bf16[128,4,8]{0,2,1:T(8,128)(2,1)S(1)}, bf16[128,4,8]{0,2,1:T(8,128)(2,1)S(1)}, u32[]{:S(2)}, u32[]{:S(2)}) %collective-permute-start.3) | collective-permute-done | bytes 8224 | tf_op jit(solution)/shard_map/while/body/eval_jaxpr/ppermute | solution.py:12
  181.2 2.9 %collective-permute-done.4 = bf16[128,1024]{0,1:T(8,128)(2,1)S(1)} collective-permute-done((bf16[128,1024]{0,1:T(8,128)(2,1)S(1)}, bf16[128,1024]{0,1:T(8,128)(2,1)S(1)}, u32[]{:S(2)}, u32[]{:S(2)}) %collective-permute-start.4) | collective-permute-done | bytes 262176 | tf_op jit(solution)/shard_map/while/body/eval_jaxpr/ppermute | solution.py:12
  185.7 1.9 collective-permute-start.2
  187.6 2.5 %collective-permute-start.3 = (bf16[128,4,8]{0,2,1:T(8,128)(2,1)S(1)}, bf16[128,4,8]{0,2,1:T(8,128)(2,1)S(1)}, u32[]{:S(2)}, u32[]{:S(2)}) collective-permute-start(bf16[128,4,8]{0,2,1:T(8,128)(2,1)S(1)} %get-tuple-element.652), channel_id=1, source_target_pairs={{4,0},{8,4},{12,8},{16,12},{20,16},{24,20},{28,24},{5,1},{9,5},{13... | collective-permute-start | bytes 24584 | tf_op jit(solution)/shard_map/while/body/eval_jaxpr/ppermute | solution.py:12
  190.1 1.9 collective-permute-start.4
  192.0 1.7 collective-permute-done.3
  194.1 3.7 %collective-permute-done.4 = bf16[128,1024]{0,1:T(8,128)(2,1)S(1)} collective-permute-done((bf16[128,1024]{0,1:T(8,128)(2,1)S(1)}, bf16[128,1024]{0,1:T(8,128)(2,1)S(1)}, u32[]{:S(2)}, u32[]{:S(2)}) %collective-permute-start.4) | collective-permute-done | bytes 262176 | tf_op jit(solution)/shard_map/while/body/eval_jaxpr/ppermute | solution.py:12
  199.5 1.9 collective-permute-start.2
  201.4 2.5 %collective-permute-start.3 = (bf16[128,4,8]{0,2,1:T(8,128)(2,1)S(1)}, bf16[128,4,8]{0,2,1:T(8,128)(2,1)S(1)}, u32[]{:S(2)}, u32[]{:S(2)}) collective-permute-start(bf16[128,4,8]{0,2,1:T(8,128)(2,1)S(1)} %get-tuple-element.652), channel_id=1, source_target_pairs={{4,0},{8,4},{12,8},{16,12},{20,16},{24,20},{28,24},{5,1},{9,5},{13... | collective-permute-start | bytes 24584 | tf_op jit(solution)/shard_map/while/body/eval_jaxpr/ppermute | solution.py:12
  203.9 1.9 collective-permute-start.4
  205.8 1.6 collective-permute-done.3
  207.8 3.7 %collective-permute-done.4 = bf16[128,1024]{0,1:T(8,128)(2,1)S(1)} collective-permute-done((bf16[128,1024]{0,1:T(8,128)(2,1)S(1)}, bf16[128,1024]{0,1:T(8,128)(2,1)S(1)}, u32[]{:S(2)}, u32[]{:S(2)}) %collective-permute-start.4) | collective-permute-done | bytes 262176 | tf_op jit(solution)/shard_map/while/body/eval_jaxpr/ppermute | solution.py:12
  213.3 1.9 collective-permute-start.2
  215.2 1.9 collective-permute-start.3
  217.1 1.9 collective-permute-start.4
  219.0 2.2 collective-permute-done.3
  221.6 3.2 %collective-permute-done.4 = bf16[128,1024]{0,1:T(8,128)(2,1)S(1)} collective-permute-done((bf16[128,1024]{0,1:T(8,128)(2,1)S(1)}, bf16[128,1024]{0,1:T(8,128)(2,1)S(1)}, u32[]{:S(2)}, u32[]{:S(2)}) %collective-permute-start.4) | collective-permute-done | bytes 262176 | tf_op jit(solution)/shard_map/while/body/eval_jaxpr/ppermute | solution.py:12
  (195 shorter events, 46.7 us)
Async XLA Ops:
  7.2 5.5 %copy-start.7 = (bf16[128,1024]{1,0:T(8,128)(2,1)S(1)}, bf16[128,1024]{1,0:T(8,128)(2,1)}, u32[]{:S(2)}) copy-start(bf16[128,1024]{1,0:T(8,128)(2,1)} %param.18) | copy-start | bytes 786436
  7.2 5.7 %copy-start.8 = (bf16[128,1024]{1,0:T(8,128)(2,1)S(1)}, bf16[128,1024]{1,0:T(8,128)(2,1)}, u32[]{:S(2)}) copy-start(bf16[128,1024]{1,0:T(8,128)(2,1)} %param.19) | copy-start | bytes 786436
  7.2 221.9 %all-gather.3.cloned.1.call-start = ((), (), s32[]{:S(2)}) async-start(), calls=%async_computation | async-start | bytes 1081344 | tf_op jit(solution)/shard_map/all_gather | solution.py:177
  9.9 3.3 %copy-start.9 = (bf16[128,1024]{1,0:T(8,128)(2,1)S(1)}, bf16[128,1024]{1,0:T(8,128)(2,1)}, u32[]{:S(2)}) copy-start(bf16[128,1024]{1,0:T(8,128)(2,1)} %param.17) | copy-start | bytes 786436
  9.9 90.7 %collective-permute-start.5 = (bf16[127,2048]{1,0:T(8,128)(2,1)}, bf16[127,2048]{1,0:T(8,128)(2,1)}, u32[]{:S(2)}, u32[]{:S(2)}) collective-permute-start(bf16[127,2048]{1,0:T(8,128)(2,1)} %bitcast.111), channel_id=1, source_target_pairs={{4,0},{8,4},{12,8},{16,12},{20,16},{24,20},{28,24},{5,1},{9,5},{13... | collective-permute-start | bytes 1560584 | tf_op jit(solution)/shard_map/ppermute | solution.py:12
  13.4 1.0 copy-start.10
  13.6 1.0 copy-start.11
  14.1 1.8 copy-start
  14.6 1.3 copy-start.2
  16.5 80.6 %copy-start.12 = (f32[64,128]{1,0:T(8,128)S(1)}, f32[64,128]{1,0:T(8,128)}, u32[]{:S(2)}) copy-start(f32[64,128]{1,0:T(8,128)} %param.25) | copy-start | bytes 98308
  16.5 6.4 %collective-permute-start = (bf16[128,1024]{0,1:T(8,128)(2,1)S(1)}, bf16[128,1024]{0,1:T(8,128)(2,1)S(1)}, u32[]{:S(2)}, u32[]{:S(2)}) collective-permute-start(bf16[128,1024]{0,1:T(8,128)(2,1)S(1)} %get-tuple-element.618), channel_id=1, source_target_pairs={{0,4},{4,8},{8,12},{12,16},{16,20},{20,24},{24,28},{1,5},{5,9},{9,... | collective-permute-start | bytes 786440 | tf_op jit(solution)/shard_map/while/body/eval_jaxpr/ppermute | solution.py:12
  19.7 6.5 %collective-permute-start.1 = (bf16[128,1024]{0,1:T(8,128)(2,1)S(1)}, bf16[128,1024]{0,1:T(8,128)(2,1)S(1)}, u32[]{:S(2)}, u32[]{:S(2)}) collective-permute-start(bf16[128,1024]{0,1:T(8,128)(2,1)S(1)} %get-tuple-element.619), channel_id=1, source_target_pairs={{0,4},{4,8},{8,12},{12,16},{16,20},{20,24},{24,28},{1,5},{5,9},{9,... | collective-permute-start | bytes 786440 | tf_op jit(solution)/shard_map/while/body/eval_jaxpr/ppermute | solution.py:12
  27.3 7.7 %collective-permute-start = (bf16[128,1024]{0,1:T(8,128)(2,1)S(1)}, bf16[128,1024]{0,1:T(8,128)(2,1)S(1)}, u32[]{:S(2)}, u32[]{:S(2)}) collective-permute-start(bf16[128,1024]{0,1:T(8,128)(2,1)S(1)} %get-tuple-element.618), channel_id=1, source_target_pairs={{0,4},{4,8},{8,12},{12,16},{16,20},{20,24},{24,28},{1,5},{5,9},{9,... | collective-permute-start | bytes 786440 | tf_op jit(solution)/shard_map/while/body/eval_jaxpr/ppermute | solution.py:12
  31.7 6.1 %collective-permute-start.1 = (bf16[128,1024]{0,1:T(8,128)(2,1)S(1)}, bf16[128,1024]{0,1:T(8,128)(2,1)S(1)}, u32[]{:S(2)}, u32[]{:S(2)}) collective-permute-start(bf16[128,1024]{0,1:T(8,128)(2,1)S(1)} %get-tuple-element.619), channel_id=1, source_target_pairs={{0,4},{4,8},{8,12},{12,16},{16,20},{20,24},{24,28},{1,5},{5,9},{9,... | collective-permute-start | bytes 786440 | tf_op jit(solution)/shard_map/while/body/eval_jaxpr/ppermute | solution.py:12
  38.9 7.7 %collective-permute-start = (bf16[128,1024]{0,1:T(8,128)(2,1)S(1)}, bf16[128,1024]{0,1:T(8,128)(2,1)S(1)}, u32[]{:S(2)}, u32[]{:S(2)}) collective-permute-start(bf16[128,1024]{0,1:T(8,128)(2,1)S(1)} %get-tuple-element.618), channel_id=1, source_target_pairs={{0,4},{4,8},{8,12},{12,16},{16,20},{20,24},{24,28},{1,5},{5,9},{9,... | collective-permute-start | bytes 786440 | tf_op jit(solution)/shard_map/while/body/eval_jaxpr/ppermute | solution.py:12
  43.3 6.1 %collective-permute-start.1 = (bf16[128,1024]{0,1:T(8,128)(2,1)S(1)}, bf16[128,1024]{0,1:T(8,128)(2,1)S(1)}, u32[]{:S(2)}, u32[]{:S(2)}) collective-permute-start(bf16[128,1024]{0,1:T(8,128)(2,1)S(1)} %get-tuple-element.619), channel_id=1, source_target_pairs={{0,4},{4,8},{8,12},{12,16},{16,20},{20,24},{24,28},{1,5},{5,9},{9,... | collective-permute-start | bytes 786440 | tf_op jit(solution)/shard_map/while/body/eval_jaxpr/ppermute | solution.py:12
  50.6 7.7 %collective-permute-start = (bf16[128,1024]{0,1:T(8,128)(2,1)S(1)}, bf16[128,1024]{0,1:T(8,128)(2,1)S(1)}, u32[]{:S(2)}, u32[]{:S(2)}) collective-permute-start(bf16[128,1024]{0,1:T(8,128)(2,1)S(1)} %get-tuple-element.618), channel_id=1, source_target_pairs={{0,4},{4,8},{8,12},{12,16},{16,20},{20,24},{24,28},{1,5},{5,9},{9,... | collective-permute-start | bytes 786440 | tf_op jit(solution)/shard_map/while/body/eval_jaxpr/ppermute | solution.py:12
  55.0 6.1 %collective-permute-start.1 = (bf16[128,1024]{0,1:T(8,128)(2,1)S(1)}, bf16[128,1024]{0,1:T(8,128)(2,1)S(1)}, u32[]{:S(2)}, u32[]{:S(2)}) collective-permute-start(bf16[128,1024]{0,1:T(8,128)(2,1)S(1)} %get-tuple-element.619), channel_id=1, source_target_pairs={{0,4},{4,8},{8,12},{12,16},{16,20},{20,24},{24,28},{1,5},{5,9},{9,... | collective-permute-start | bytes 786440 | tf_op jit(solution)/shard_map/while/body/eval_jaxpr/ppermute | solution.py:12
  62.2 7.7 %collective-permute-start = (bf16[128,1024]{0,1:T(8,128)(2,1)S(1)}, bf16[128,1024]{0,1:T(8,128)(2,1)S(1)}, u32[]{:S(2)}, u32[]{:S(2)}) collective-permute-start(bf16[128,1024]{0,1:T(8,128)(2,1)S(1)} %get-tuple-element.618), channel_id=1, source_target_pairs={{0,4},{4,8},{8,12},{12,16},{16,20},{20,24},{24,28},{1,5},{5,9},{9,... | collective-permute-start | bytes 786440 | tf_op jit(solution)/shard_map/while/body/eval_jaxpr/ppermute | solution.py:12
  66.6 6.1 %collective-permute-start.1 = (bf16[128,1024]{0,1:T(8,128)(2,1)S(1)}, bf16[128,1024]{0,1:T(8,128)(2,1)S(1)}, u32[]{:S(2)}, u32[]{:S(2)}) collective-permute-start(bf16[128,1024]{0,1:T(8,128)(2,1)S(1)} %get-tuple-element.619), channel_id=1, source_target_pairs={{0,4},{4,8},{8,12},{12,16},{16,20},{20,24},{24,28},{1,5},{5,9},{9,... | collective-permute-start | bytes 786440 | tf_op jit(solution)/shard_map/while/body/eval_jaxpr/ppermute | solution.py:12
  73.8 7.7 %collective-permute-start = (bf16[128,1024]{0,1:T(8,128)(2,1)S(1)}, bf16[128,1024]{0,1:T(8,128)(2,1)S(1)}, u32[]{:S(2)}, u32[]{:S(2)}) collective-permute-start(bf16[128,1024]{0,1:T(8,128)(2,1)S(1)} %get-tuple-element.618), channel_id=1, source_target_pairs={{0,4},{4,8},{8,12},{12,16},{16,20},{20,24},{24,28},{1,5},{5,9},{9,... | collective-permute-start | bytes 786440 | tf_op jit(solution)/shard_map/while/body/eval_jaxpr/ppermute | solution.py:12
  78.2 6.1 %collective-permute-start.1 = (bf16[128,1024]{0,1:T(8,128)(2,1)S(1)}, bf16[128,1024]{0,1:T(8,128)(2,1)S(1)}, u32[]{:S(2)}, u32[]{:S(2)}) collective-permute-start(bf16[128,1024]{0,1:T(8,128)(2,1)S(1)} %get-tuple-element.619), channel_id=1, source_target_pairs={{0,4},{4,8},{8,12},{12,16},{16,20},{20,24},{24,28},{1,5},{5,9},{9,... | collective-permute-start | bytes 786440 | tf_op jit(solution)/shard_map/while/body/eval_jaxpr/ppermute | solution.py:12
  85.4 7.7 %collective-permute-start = (bf16[128,1024]{0,1:T(8,128)(2,1)S(1)}, bf16[128,1024]{0,1:T(8,128)(2,1)S(1)}, u32[]{:S(2)}, u32[]{:S(2)}) collective-permute-start(bf16[128,1024]{0,1:T(8,128)(2,1)S(1)} %get-tuple-element.618), channel_id=1, source_target_pairs={{0,4},{4,8},{8,12},{12,16},{16,20},{20,24},{24,28},{1,5},{5,9},{9,... | collective-permute-start | bytes 786440 | tf_op jit(solution)/shard_map/while/body/eval_jaxpr/ppermute | solution.py:12
  89.8 6.1 %collective-permute-start.1 = (bf16[128,1024]{0,1:T(8,128)(2,1)S(1)}, bf16[128,1024]{0,1:T(8,128)(2,1)S(1)}, u32[]{:S(2)}, u32[]{:S(2)}) collective-permute-start(bf16[128,1024]{0,1:T(8,128)(2,1)S(1)} %get-tuple-element.619), channel_id=1, source_target_pairs={{0,4},{4,8},{8,12},{12,16},{16,20},{20,24},{24,28},{1,5},{5,9},{9,... | collective-permute-start | bytes 786440 | tf_op jit(solution)/shard_map/while/body/eval_jaxpr/ppermute | solution.py:12
  99.2 1.0 copy-start.1
  99.2 1.1 copy-start.3
  100.6 1.5 copy-start.4
  102.1 11.4 %copy-start.5 = (bf16[128,2048]{1,0:T(8,128)(2,1)S(1)}, bf16[128,2048]{1,0:T(8,128)(2,1)}, u32[]{:S(2)}) copy-start(bf16[128,2048]{1,0:T(8,128)(2,1)} %param.21) | copy-start | bytes 1572868
  102.1 11.4 %copy-start.6 = (bf16[128,2048]{1,0:T(8,128)(2,1)S(1)}, bf16[128,2048]{1,0:T(8,128)(2,1)}, u32[]{:S(2)}) copy-start(bf16[128,2048]{1,0:T(8,128)(2,1)} %param.22) | copy-start | bytes 1572868
  130.4 8.7 %collective-permute-start.2 = (bf16[128,1024]{0,1:T(8,128)(2,1)}, bf16[128,1024]{0,1:T(8,128)(2,1)S(1)}, u32[]{:S(2)}, u32[]{:S(2)}) collective-permute-start(bf16[128,1024]{0,1:T(8,128)(2,1)} %get-tuple-element.650), channel_id=1, source_target_pairs={{4,0},{8,4},{12,8},{16,12},{20,16},{24,20},{28,24},{5,1},{9,5},{13... | collective-permute-start | bytes 786440 | tf_op jit(solution)/shard_map/while/body/eval_jaxpr/ppermute | solution.py:12
  133.2 5.9 %collective-permute-start.3 = (bf16[128,4,8]{0,2,1:T(8,128)(2,1)S(1)}, bf16[128,4,8]{0,2,1:T(8,128)(2,1)S(1)}, u32[]{:S(2)}, u32[]{:S(2)}) collective-permute-start(bf16[128,4,8]{0,2,1:T(8,128)(2,1)S(1)} %get-tuple-element.652), channel_id=1, source_target_pairs={{4,0},{8,4},{12,8},{16,12},{20,16},{24,20},{28,24},{5,1},{9,5},{13... | collective-permute-start | bytes 24584 | tf_op jit(solution)/shard_map/while/body/eval_jaxpr/ppermute | solution.py:12
  135.1 8.1 %collective-permute-start.4 = (bf16[128,1024]{0,1:T(8,128)(2,1)S(1)}, bf16[128,1024]{0,1:T(8,128)(2,1)S(1)}, u32[]{:S(2)}, u32[]{:S(2)}) collective-permute-start(bf16[128,1024]{0,1:T(8,128)(2,1)S(1)} %get-tuple-element.651), channel_id=1, source_target_pairs={{4,0},{8,4},{12,8},{16,12},{20,16},{24,20},{28,24},{5,1},{9,5},{13... | collective-permute-start | bytes 786440 | tf_op jit(solution)/shard_map/while/body/eval_jaxpr/ppermute | solution.py:12
  144.9 8.1 %collective-permute-start.2 = (bf16[128,1024]{0,1:T(8,128)(2,1)}, bf16[128,1024]{0,1:T(8,128)(2,1)S(1)}, u32[]{:S(2)}, u32[]{:S(2)}) collective-permute-start(bf16[128,1024]{0,1:T(8,128)(2,1)} %get-tuple-element.650), channel_id=1, source_target_pairs={{4,0},{8,4},{12,8},{16,12},{20,16},{24,20},{28,24},{5,1},{9,5},{13... | collective-permute-start | bytes 786440 | tf_op jit(solution)/shard_map/while/body/eval_jaxpr/ppermute | solution.py:12
  146.8 6.2 %collective-permute-start.3 = (bf16[128,4,8]{0,2,1:T(8,128)(2,1)S(1)}, bf16[128,4,8]{0,2,1:T(8,128)(2,1)S(1)}, u32[]{:S(2)}, u32[]{:S(2)}) collective-permute-start(bf16[128,4,8]{0,2,1:T(8,128)(2,1)S(1)} %get-tuple-element.652), channel_id=1, source_target_pairs={{4,0},{8,4},{12,8},{16,12},{20,16},{24,20},{28,24},{5,1},{9,5},{13... | collective-permute-start | bytes 24584 | tf_op jit(solution)/shard_map/while/body/eval_jaxpr/ppermute | solution.py:12
  148.9 7.7 %collective-permute-start.4 = (bf16[128,1024]{0,1:T(8,128)(2,1)S(1)}, bf16[128,1024]{0,1:T(8,128)(2,1)S(1)}, u32[]{:S(2)}, u32[]{:S(2)}) collective-permute-start(bf16[128,1024]{0,1:T(8,128)(2,1)S(1)} %get-tuple-element.651), channel_id=1, source_target_pairs={{4,0},{8,4},{12,8},{16,12},{20,16},{24,20},{28,24},{5,1},{9,5},{13... | collective-permute-start | bytes 786440 | tf_op jit(solution)/shard_map/while/body/eval_jaxpr/ppermute | solution.py:12
  158.2 8.8 %collective-permute-start.2 = (bf16[128,1024]{0,1:T(8,128)(2,1)}, bf16[128,1024]{0,1:T(8,128)(2,1)S(1)}, u32[]{:S(2)}, u32[]{:S(2)}) collective-permute-start(bf16[128,1024]{0,1:T(8,128)(2,1)} %get-tuple-element.650), channel_id=1, source_target_pairs={{4,0},{8,4},{12,8},{16,12},{20,16},{24,20},{28,24},{5,1},{9,5},{13... | collective-permute-start | bytes 786440 | tf_op jit(solution)/shard_map/while/body/eval_jaxpr/ppermute | solution.py:12
  160.1 6.9 %collective-permute-start.3 = (bf16[128,4,8]{0,2,1:T(8,128)(2,1)S(1)}, bf16[128,4,8]{0,2,1:T(8,128)(2,1)S(1)}, u32[]{:S(2)}, u32[]{:S(2)}) collective-permute-start(bf16[128,4,8]{0,2,1:T(8,128)(2,1)S(1)} %get-tuple-element.652), channel_id=1, source_target_pairs={{4,0},{8,4},{12,8},{16,12},{20,16},{24,20},{28,24},{5,1},{9,5},{13... | collective-permute-start | bytes 24584 | tf_op jit(solution)/shard_map/while/body/eval_jaxpr/ppermute | solution.py:12
  162.1 7.7 %collective-permute-start.4 = (bf16[128,1024]{0,1:T(8,128)(2,1)S(1)}, bf16[128,1024]{0,1:T(8,128)(2,1)S(1)}, u32[]{:S(2)}, u32[]{:S(2)}) collective-permute-start(bf16[128,1024]{0,1:T(8,128)(2,1)S(1)} %get-tuple-element.651), channel_id=1, source_target_pairs={{4,0},{8,4},{12,8},{16,12},{20,16},{24,20},{28,24},{5,1},{9,5},{13... | collective-permute-start | bytes 786440 | tf_op jit(solution)/shard_map/while/body/eval_jaxpr/ppermute | solution.py:12
  171.4 9.4 %collective-permute-start.2 = (bf16[128,1024]{0,1:T(8,128)(2,1)}, bf16[128,1024]{0,1:T(8,128)(2,1)S(1)}, u32[]{:S(2)}, u32[]{:S(2)}) collective-permute-start(bf16[128,1024]{0,1:T(8,128)(2,1)} %get-tuple-element.650), channel_id=1, source_target_pairs={{4,0},{8,4},{12,8},{16,12},{20,16},{24,20},{28,24},{5,1},{9,5},{13... | collective-permute-start | bytes 786440 | tf_op jit(solution)/shard_map/while/body/eval_jaxpr/ppermute | solution.py:12
  173.4 7.5 %collective-permute-start.3 = (bf16[128,4,8]{0,2,1:T(8,128)(2,1)S(1)}, bf16[128,4,8]{0,2,1:T(8,128)(2,1)S(1)}, u32[]{:S(2)}, u32[]{:S(2)}) collective-permute-start(bf16[128,4,8]{0,2,1:T(8,128)(2,1)S(1)} %get-tuple-element.652), channel_id=1, source_target_pairs={{4,0},{8,4},{12,8},{16,12},{20,16},{24,20},{28,24},{5,1},{9,5},{13... | collective-permute-start | bytes 24584 | tf_op jit(solution)/shard_map/while/body/eval_jaxpr/ppermute | solution.py:12
  175.4 8.6 %collective-permute-start.4 = (bf16[128,1024]{0,1:T(8,128)(2,1)S(1)}, bf16[128,1024]{0,1:T(8,128)(2,1)S(1)}, u32[]{:S(2)}, u32[]{:S(2)}) collective-permute-start(bf16[128,1024]{0,1:T(8,128)(2,1)S(1)} %get-tuple-element.651), channel_id=1, source_target_pairs={{4,0},{8,4},{12,8},{16,12},{20,16},{24,20},{28,24},{5,1},{9,5},{13... | collective-permute-start | bytes 786440 | tf_op jit(solution)/shard_map/while/body/eval_jaxpr/ppermute | solution.py:12
  185.7 8.0 %collective-permute-start.2 = (bf16[128,1024]{0,1:T(8,128)(2,1)}, bf16[128,1024]{0,1:T(8,128)(2,1)S(1)}, u32[]{:S(2)}, u32[]{:S(2)}) collective-permute-start(bf16[128,1024]{0,1:T(8,128)(2,1)} %get-tuple-element.650), channel_id=1, source_target_pairs={{4,0},{8,4},{12,8},{16,12},{20,16},{24,20},{28,24},{5,1},{9,5},{13... | collective-permute-start | bytes 786440 | tf_op jit(solution)/shard_map/while/body/eval_jaxpr/ppermute | solution.py:12
  187.6 6.1 %collective-permute-start.3 = (bf16[128,4,8]{0,2,1:T(8,128)(2,1)S(1)}, bf16[128,4,8]{0,2,1:T(8,128)(2,1)S(1)}, u32[]{:S(2)}, u32[]{:S(2)}) collective-permute-start(bf16[128,4,8]{0,2,1:T(8,128)(2,1)S(1)} %get-tuple-element.652), channel_id=1, source_target_pairs={{4,0},{8,4},{12,8},{16,12},{20,16},{24,20},{28,24},{5,1},{9,5},{13... | collective-permute-start | bytes 24584 | tf_op jit(solution)/shard_map/while/body/eval_jaxpr/ppermute | solution.py:12
  190.1 7.7 %collective-permute-start.4 = (bf16[128,1024]{0,1:T(8,128)(2,1)S(1)}, bf16[128,1024]{0,1:T(8,128)(2,1)S(1)}, u32[]{:S(2)}, u32[]{:S(2)}) collective-permute-start(bf16[128,1024]{0,1:T(8,128)(2,1)S(1)} %get-tuple-element.651), channel_id=1, source_target_pairs={{4,0},{8,4},{12,8},{16,12},{20,16},{24,20},{28,24},{5,1},{9,5},{13... | collective-permute-start | bytes 786440 | tf_op jit(solution)/shard_map/while/body/eval_jaxpr/ppermute | solution.py:12
  199.5 8.0 %collective-permute-start.2 = (bf16[128,1024]{0,1:T(8,128)(2,1)}, bf16[128,1024]{0,1:T(8,128)(2,1)S(1)}, u32[]{:S(2)}, u32[]{:S(2)}) collective-permute-start(bf16[128,1024]{0,1:T(8,128)(2,1)} %get-tuple-element.650), channel_id=1, source_target_pairs={{4,0},{8,4},{12,8},{16,12},{20,16},{24,20},{28,24},{5,1},{9,5},{13... | collective-permute-start | bytes 786440 | tf_op jit(solution)/shard_map/while/body/eval_jaxpr/ppermute | solution.py:12
  201.4 6.1 %collective-permute-start.3 = (bf16[128,4,8]{0,2,1:T(8,128)(2,1)S(1)}, bf16[128,4,8]{0,2,1:T(8,128)(2,1)S(1)}, u32[]{:S(2)}, u32[]{:S(2)}) collective-permute-start(bf16[128,4,8]{0,2,1:T(8,128)(2,1)S(1)} %get-tuple-element.652), channel_id=1, source_target_pairs={{4,0},{8,4},{12,8},{16,12},{20,16},{24,20},{28,24},{5,1},{9,5},{13... | collective-permute-start | bytes 24584 | tf_op jit(solution)/shard_map/while/body/eval_jaxpr/ppermute | solution.py:12
  203.9 7.7 %collective-permute-start.4 = (bf16[128,1024]{0,1:T(8,128)(2,1)S(1)}, bf16[128,1024]{0,1:T(8,128)(2,1)S(1)}, u32[]{:S(2)}, u32[]{:S(2)}) collective-permute-start(bf16[128,1024]{0,1:T(8,128)(2,1)S(1)} %get-tuple-element.651), channel_id=1, source_target_pairs={{4,0},{8,4},{12,8},{16,12},{20,16},{24,20},{28,24},{5,1},{9,5},{13... | collective-permute-start | bytes 786440 | tf_op jit(solution)/shard_map/while/body/eval_jaxpr/ppermute | solution.py:12
  213.3 8.0 %collective-permute-start.2 = (bf16[128,1024]{0,1:T(8,128)(2,1)}, bf16[128,1024]{0,1:T(8,128)(2,1)S(1)}, u32[]{:S(2)}, u32[]{:S(2)}) collective-permute-start(bf16[128,1024]{0,1:T(8,128)(2,1)} %get-tuple-element.650), channel_id=1, source_target_pairs={{4,0},{8,4},{12,8},{16,12},{20,16},{24,20},{28,24},{5,1},{9,5},{13... | collective-permute-start | bytes 786440 | tf_op jit(solution)/shard_map/while/body/eval_jaxpr/ppermute | solution.py:12
  215.2 6.1 %collective-permute-start.3 = (bf16[128,4,8]{0,2,1:T(8,128)(2,1)S(1)}, bf16[128,4,8]{0,2,1:T(8,128)(2,1)S(1)}, u32[]{:S(2)}, u32[]{:S(2)}) collective-permute-start(bf16[128,4,8]{0,2,1:T(8,128)(2,1)S(1)} %get-tuple-element.652), channel_id=1, source_target_pairs={{4,0},{8,4},{12,8},{16,12},{20,16},{24,20},{28,24},{5,1},{9,5},{13... | collective-permute-start | bytes 24584 | tf_op jit(solution)/shard_map/while/body/eval_jaxpr/ppermute | solution.py:12
  217.1 7.7 %collective-permute-start.4 = (bf16[128,1024]{0,1:T(8,128)(2,1)S(1)}, bf16[128,1024]{0,1:T(8,128)(2,1)S(1)}, u32[]{:S(2)}, u32[]{:S(2)}) collective-permute-start(bf16[128,1024]{0,1:T(8,128)(2,1)S(1)} %get-tuple-element.651), channel_id=1, source_target_pairs={{4,0},{8,4},{12,8},{16,12},{20,16},{24,20},{28,24},{5,1},{9,5},{13... | collective-permute-start | bytes 786440 | tf_op jit(solution)/shard_map/while/body/eval_jaxpr/ppermute | solution.py:12
Sparse Core Ops, SparseCore 0:
  130.5 54.3 all-gather.2
